TPU v7x, 256 devices: a whole 4x4x8 slice. The times are simulated.
256 devices in a mesh: dist: 2 (over core), rows: 128 (over y, z, x).
Axes of the slice: x: 4, y: 4, z: 8, core: 2. Of those that a mesh axis runs over, the one named last changes fastest.
Arguments:
- holograms: bfloat16 [1, 4, 4, 1024, 1024], P(None, None, 'dist', 'rows'), may hold values from -6 to 6
- propagation: float32 [4], replicated, may hold values from 100 to 1000
- weights: bfloat16 [4, 1024, 1024], P(None, None, 'dist'), may hold values from -0.09375 to 0.09375
- angle_order: int32 [1, 4], replicated, may hold values from 0 to 3, each once within a row
- slab_rows: int32 [128], replicated, may hold values from 0 to 16, as said below
Outputs:
- slab: bfloat16 [2048, 1024], P('rows', 'dist')
Inputs may be any that keep to these rules, and one draw needn't show every extreme that they name: Owners 2j and 2j+1 together own 16 slices: slab_rows[2j] + slab_rows[2j+1] = 16, so owner 2j holds slices 2j 8 onward and owner 2j+1 the rest of that pair's range; in every draw some owner holds 16.
All inputs are finite; a program needn't handle non-finite values.
Results may differ from a plain program's by a relative error of at most 0.02.
Values may be sent and summed in bfloat16 or wider, within the bound.
A program may use at most 128 MiB of HBM per device.

v0:
```python
import math

import jax
import jax.numpy as jnp
from jax import lax
from jax.sharding import PartitionSpec as P

absorb_ratio = 0.1
regularizer = 0.05


def swapped(value, axis, bit):
    mask = 2**bit
    pairs = [(source, source ^ mask) for source in range(lax.axis_size(axis))]
    return lax.ppermute(value, axis, pairs)


def dft_tables(length):
    index = jnp.arange(length, dtype=jnp.int32)
    product = index[:, None] * index[None, :] % length
    turned = product.astype(jnp.float32) * (2.0 * math.pi / length)
    factor = 1.0 / math.sqrt(length)
    return (
        (jnp.cos(turned) * factor).astype(jnp.bfloat16),
        (jnp.sin(turned) * factor).astype(jnp.bfloat16),
    )


def on_device(holograms, propagation, weights, angle_order, slab_rows):
    mbatch, angles, dist_dev, rows_dev, width = holograms.shape
    groups = lax.axis_size("rows")
    capacity = 2 * rows_dev
    cosine, sine = dft_tables(width)
    col_cos = cosine.reshape(groups, rows_dev, width)
    col_sin = sine.reshape(groups, rows_dev, width)
    index = jnp.arange(width, dtype=jnp.int32)
    signed = jnp.where(index < width // 2, index, index - width).astype(jnp.float32)
    device = lax.axis_index("rows")
    local_freq = lax.dynamic_slice_in_dim(signed, device * rows_dev, rows_dev, 0)
    radius = (local_freq[:, None] ** 2 + signed[None, :] ** 2) / float(width * width)
    chirp = propagation[:, None, None] * radius[None]
    transfer = 2.0 * (jnp.sin(chirp) + absorb_ratio * jnp.cos(chirp))
    denom = jnp.sum(transfer * transfer, axis=0) + regularizer
    mine = lax.dynamic_slice_in_dim(transfer, lax.axis_index("dist") * dist_dev, dist_dev, 0)
    parity = device % 2
    offset = parity * slab_rows[device - parity]
    count = slab_rows[device]
    slot = jnp.arange(capacity, dtype=jnp.int32)[:, None]
    source = jnp.arange(capacity, dtype=jnp.int32)[None, :]
    select = ((source == offset + slot) & (slot < count)).astype(jnp.float32)
    flat = holograms[0].reshape(angles * dist_dev * rows_dev, width)
    row_re = jnp.dot(flat, cosine, preferred_element_type=jnp.float32).astype(jnp.bfloat16)
    row_im = (-jnp.dot(flat, sine, preferred_element_type=jnp.float32)).astype(jnp.bfloat16)
    row_re = row_re.reshape(angles * dist_dev, rows_dev, width)
    row_im = row_im.reshape(angles * dist_dev, rows_dev, width)
    pieces = (
        lax.all_to_all(row_re, "rows", split_axis=2, concat_axis=2, tiled=True),
        lax.all_to_all(row_im, "rows", split_axis=2, concat_axis=2, tiled=True),
    )
    items = pieces[0].shape[0]
    real_part = pieces[0].reshape(items, rows_dev, groups, rows_dev)
    imag_part = pieces[1].reshape(items, rows_dev, groups, rows_dev)
    out_re = jnp.einsum("aysk,syq->akq", real_part, col_cos, preferred_element_type=jnp.float32)
    out_re = out_re + jnp.einsum(
        "aysk,syq->akq", imag_part, col_sin, preferred_element_type=jnp.float32
    )
    out_im = jnp.einsum("aysk,syq->akq", imag_part, col_cos, preferred_element_type=jnp.float32)
    out_im = out_im - jnp.einsum(
        "aysk,syq->akq", real_part, col_sin, preferred_element_type=jnp.float32
    )
    spec_re = out_re
    spec_im = out_im
    spec_re = spec_re.reshape(angles, dist_dev, rows_dev, width)
    spec_im = spec_im.reshape(angles, dist_dev, rows_dev, width)
    numer_re = jnp.sum(mine[None] * spec_re, axis=1)
    numer_im = jnp.sum(mine[None] * spec_im, axis=1)
    numer_re, numer_im = (
        lax.psum(numer_re.astype(jnp.bfloat16), "dist").astype(jnp.float32),
        lax.psum(numer_im.astype(jnp.bfloat16), "dist").astype(jnp.float32),
    )
    spec_phase_re = (numer_re / denom).astype(jnp.bfloat16)
    spec_phase_im = (numer_im / denom).astype(jnp.bfloat16)
    half_re = jnp.einsum("akq,qy->aky", spec_phase_re, cosine, preferred_element_type=jnp.float32)
    half_re = (
        half_re - jnp.einsum("akq,qy->aky", spec_phase_im, sine, preferred_element_type=jnp.float32)
    ).astype(jnp.bfloat16)
    half_im = jnp.einsum("akq,qy->aky", spec_phase_im, cosine, preferred_element_type=jnp.float32)
    half_im = (
        half_im + jnp.einsum("akq,qy->aky", spec_phase_re, sine, preferred_element_type=jnp.float32)
    ).astype(jnp.bfloat16)
    pieces = (
        lax.all_to_all(half_re, "rows", split_axis=2, concat_axis=2, tiled=True),
        lax.all_to_all(half_im, "rows", split_axis=2, concat_axis=2, tiled=True),
    )
    items = pieces[0].shape[0]
    real_part = pieces[0].reshape(items, rows_dev, groups, rows_dev)
    imag_part = pieces[1].reshape(items, rows_dev, groups, rows_dev)
    result = jnp.einsum("aksy,skx->ayx", real_part, col_cos, preferred_element_type=jnp.float32)
    phase = (
        result - jnp.einsum("aksy,skx->ayx", imag_part, col_sin, preferred_element_type=jnp.float32)
    ).astype(jnp.bfloat16)
    chosen = weights[0 + angle_order[0]]
    partner = swapped(phase, "rows", 0)
    lower = jnp.where(parity == 1, partner, phase)
    upper = jnp.where(parity == 1, phase, partner)
    paired = jnp.concatenate([lower, upper], axis=1)
    rows_in = jnp.einsum(
        "ij,ajx->aix", select.astype(jnp.bfloat16), paired, preferred_element_type=jnp.float32
    ).astype(jnp.bfloat16)
    recon = jnp.einsum("ayx,axp->yp", rows_in, chosen, preferred_element_type=jnp.float32)
    return recon.astype(jnp.bfloat16)


def solution(mesh):
    return jax.shard_map(
        on_device,
        mesh=mesh,
        in_specs=(P(None, None, "dist", "rows", None), P(), P(None, None, "dist"), P(), P()),
        out_specs=P("rows", "dist"),
        check_vma=False,
    )
```

profile of v0, /device:TPU:2, one launch (start us, length us, event | category | flops | bytes accessed | tf_op | source)
XLA Modules:
  0.0 350.8 jit_solution(18105776519220072496)
XLA Ops:
  7.4 16.1 %fusion.66 = bf16[8,8,1024]{2,1,0:T(8,128)(2,1)S(1)} fusion(bf16[64,1024]{1,0:T(8,128)(2,1)S(1)} %bitcast.132), kind=kOutput, calls=%fused_computation.56 | convolution fusion | flops 151126016 | bytes 262144 | tf_op jit(solution)/shard_map/dot_general | solution.py:53
  25.1 2.9 reshape.156
  28.0 15.8 %all-to-all-start.1 = ((bf16[128,2,256]{2,1,0:T(2,128)(2,1)}), bf16[128,2,256]{2,1,0:T(2,128)(2,1)S(1)}, u32[]{:S(2)}, u32[]{:S(2)}) async-start(bf16[128,2,256]{2,1,0:T(2,128)(2,1)} %reshape.156), calls=%async_computation.1 | async-start | bytes 262144 | tf_op jit(solution)/shard_map/all_to_all | solution.py:58
  43.8 16.0 %fusion.65 = bf16[8,8,1024]{2,1,0:T(8,128)(2,1)S(1)} fusion(bf16[64,1024]{1,0:T(8,128)(2,1)S(1)} %bitcast.133), kind=kOutput, calls=%fused_computation.55 | convolution fusion | flops 151060480 | bytes 262144 | tf_op jit(solution)/shard_map/dot_general | solution.py:52
  61.3 2.9 reshape.154
  65.0 13.8 %all-to-all-start = ((bf16[128,2,256]{2,1,0:T(2,128)(2,1)}), bf16[128,2,256]{2,1,0:T(2,128)(2,1)S(1)}, u32[]{:S(2)}, u32[]{:S(2)}) async-start(bf16[128,2,256]{2,1,0:T(2,128)(2,1)} %reshape.154), calls=%async_computation | async-start | bytes 262144 | tf_op jit(solution)/shard_map/all_to_all | solution.py:57
  78.8 3.5 reshape.157
  82.3 4.3 %copy.30 = bf16[8,8,128,8]{3,2,1,0:T(8,128)(2,1)S(1)} copy(bf16[8,8,128,8]{1,0,3,2:T(8,128)(2,1)} %bitcast.136) | data formatting | bytes 262144 | tf_op jit(solution)/shard_map/reshape | solution.py:62
  86.6 3.6 %all-to-all-done = bf16[128,2,256]{2,1,0:T(2,128)(2,1)S(1)} async-done(((bf16[128,2,256]{2,1,0:T(2,128)(2,1)}), bf16[128,2,256]{2,1,0:T(2,128)(2,1)S(1)}, u32[]{:S(2)}, u32[]{:S(2)}) %all-to-all-start) | async-done | bytes 131104 | tf_op jit(solution)/shard_map/all_to_all | solution.py:57
  90.3 3.5 reshape.155
  93.7 5.4 %copy.28 = bf16[8,8,128,8]{3,2,1,0:T(8,128)(2,1)} copy(bf16[8,8,128,8]{1,0,3,2:T(8,128)(2,1)} %bitcast.137) | data formatting | bytes 262144 | tf_op jit(solution)/shard_map/reshape | solution.py:61
  99.1 16.0 %fusion.39 = f32[8,8,1024]{2,1,0:T(8,128)S(1)} fusion(bf16[8,8,128,8]{3,2,1,0:T(8,128)(2,1)S(1)} %copy.30, s32[128,8]{0,1:T(8,128)S(1)} %multiply_add_fusion), kind=kOutput, calls=%fused_computation.42 | convolution fusion | flops 150994944 | bytes 397312 | tf_op jit(solution)/shard_map/aysk,syq->akq/dot_general | solution.py:67
  115.2 16.1 %fusion.36 = f32[8,8,1024]{2,1,0:T(8,128)S(1)} fusion(bf16[8,8,128,8]{3,2,1,0:T(8,128)(2,1)S(1)} %copy-done.1, s32[128,8]{0,1:T(8,128)S(1)} %multiply_add_fusion), kind=kOutput, calls=%fused_computation.41 | convolution fusion | flops 150994944 | bytes 397312 | tf_op jit(solution)/shard_map/aysk,syq->akq/dot_general | solution.py:63
  131.2 16.5 %fusion.48 = f32[8,8,1024]{2,1,0:T(8,128)S(1)} fusion(f32[8,8,1024]{2,1,0:T(8,128)S(1)} %fusion.39, bf16[8,8,128,8]{3,2,1,0:T(8,128)(2,1)S(1)} %copy-done.1, s32[128,8]{0,1:T(8,128)S(1)} %multiply_add_fusion), kind=kOutput, calls=%fused_computation.45 | convolution fusion | flops 151060480 | bytes 659456 | tf_op jit(solution)/shard_map/aysk,syq->akq/dot_general | solution.py:68
  147.8 16.8 %multiply_reduce_fusion.1 = (bf16[4,8,1024]{2,1,0:T(8,128)(2,1)}, bf16[4,8,1024]{2,1,0:T(8,128)(2,1)}) fusion(f32[2,8,1024]{2,1,0:T(8,128)S(1)} %constant_dynamic-slice_fusion, f32[8,8,1024]{2,1,0:T(8,128)S(1)} %fusion.48, f32[8,8,1024]{2,1,0:T(8,128)S(1)} %fusion.36, bf16[8,8,128,8]{3,2,1,0:T(8,128)(2,1)S(1)} %copy.30, s32[128,8]{0,1:T(8,128)S(1)} %multiply_add_fusion), kind=kOutput, calls=%fused_computation.66 | convolution fusion | flops 151257088 | bytes 856064 | tf_op jit(solution)/shard_map/aysk,syq->akq/dot_general | solution.py:64
  164.6 26.7 %all-reduce.3.cloned.1.call-done = (bf16[4,8,1024]{2,1,0:T(8,128)(2,1)}, bf16[4,8,1024]{2,1,0:T(8,128)(2,1)}) async-done(((bf16[4,8,1024]{2,1,0:T(8,128)(2,1)}, bf16[4,8,1024]{2,1,0:T(8,128)(2,1)}), (bf16[4,8,1024]{2,1,0:T(8,128)(2,1)}, bf16[4,8,1024]{2,1,0:T(8,128)(2,1)})) %all-reduce.3.cloned.1.call-update) | async-done | bytes 131088 | tf_op jit(solution)/shard_map/psum | solution.py:79
  191.3 16.9 %fusion.14 = f32[4,8,1024]{2,1,0:T(8,128)S(1)} fusion(bf16[4,8,1024]{2,1,0:T(8,128)(2,1)} %get-tuple-element.8, f32[8,1024]{1,0:T(8,128)S(1)} %broadcast_add_fusion), kind=kOutput, calls=%fused_computation.25 | convolution fusion | flops 83984384 | bytes 229376 | tf_op jit(solution)/shard_map/akq,qy->aky/dot_general | solution.py:89
  208.2 16.1 %fusion.16 = f32[4,8,1024]{2,1,0:T(8,128)S(1)} fusion(bf16[4,8,1024]{2,1,0:T(8,128)(2,1)S(1)} %copy-done.5, f32[8,1024]{1,0:T(8,128)S(1)} %broadcast_add_fusion), kind=kOutput, calls=%fused_computation.27 | convolution fusion | flops 83984384 | bytes 229376 | tf_op jit(solution)/shard_map/akq,qy->aky/dot_general | solution.py:85
  224.3 15.9 %fusion.79 = bf16[4,8,1024]{2,1,0:T(8,128)(2,1)S(1)} fusion(f32[4,8,1024]{2,1,0:T(8,128)S(1)} %fusion.14, bf16[4,8,1024]{2,1,0:T(8,128)(2,1)S(1)} %copy-done.5, f32[8,1024]{1,0:T(8,128)S(1)} %broadcast_add_fusion), kind=kOutput, calls=%fused_computation.61 | convolution fusion | flops 84049920 | bytes 294912 | tf_op jit(solution)/shard_map/akq,qy->aky/dot_general | solution.py:87
  240.9 1.7 reshape.160
  242.6 14.3 %all-to-all-start.3 = ((bf16[128,2,128]{2,1,0:T(2,128)(2,1)}), bf16[128,2,128]{2,1,0:T(2,128)(2,1)S(1)}, u32[]{:S(2)}, u32[]{:S(2)}) async-start(bf16[128,2,128]{2,1,0:T(2,128)(2,1)} %reshape.160), calls=%async_computation.3 | async-start | bytes 131072 | tf_op jit(solution)/shard_map/all_to_all | solution.py:93
  257.0 15.9 %fusion.82 = bf16[4,8,1024]{2,1,0:T(8,128)(2,1)S(1)} fusion(f32[4,8,1024]{2,1,0:T(8,128)S(1)} %fusion.16, bf16[4,8,1024]{2,1,0:T(8,128)(2,1)S(1)} %copy-done.4, f32[8,1024]{1,0:T(8,128)S(1)} %broadcast_add_fusion), kind=kOutput, calls=%fused_computation.62 | convolution fusion | flops 84049920 | bytes 294912 | tf_op jit(solution)/shard_map/akq,qy->aky/dot_general | solution.py:83
  273.6 1.7 reshape.158
  275.3 13.8 %all-to-all-start.2 = ((bf16[128,2,128]{2,1,0:T(2,128)(2,1)}), bf16[128,2,128]{2,1,0:T(2,128)(2,1)S(1)}, u32[]{:S(2)}, u32[]{:S(2)}) async-start(bf16[128,2,128]{2,1,0:T(2,128)(2,1)} %reshape.158), calls=%async_computation.2 | async-start | bytes 131072 | tf_op jit(solution)/shard_map/all_to_all | solution.py:92
  290.3 5.0 %gather_fusion = bf16[4,1024,512]{2,1,0:T(8,128)(2,1)} fusion(bf16[4,1024,512]{2,1,0:T(8,128)(2,1)} %param.7, s32[1024]{0:T(1024)S(1)} %pad_clamp_fusion), kind=kCustom, calls=%fused_computation | custom fusion | bytes 8388624 | tf_op jit(solution)/shard_map/gather | solution.py:102
  296.4 2.1 copy.38
  298.5 1.8 all-to-all-done.2
  301.4 2.2 copy.36
  303.7 15.8 %fusion.57 = f32[4,8,1024]{2,1,0:T(8,128)S(1)} fusion(bf16[4,8,128,8]{3,2,1,0:T(8,128)(2,1)S(1)} %copy.36, s32[128,8]{0,1:T(8,128)S(1)} %multiply_add_fusion), kind=kOutput, calls=%fused_computation.51 | convolution fusion | flops 83886080 | bytes 200704 | tf_op jit(solution)/shard_map/aksy,skx->ayx/dot_general | solution.py:98
  319.5 16.0 %fusion.76 = bf16[4,8,1024]{2,1,0:T(8,128)(2,1)S(1)} fusion(f32[4,8,1024]{2,1,0:T(8,128)S(1)} %fusion.57, bf16[4,8,128,8]{3,2,1,0:T(8,128)(2,1)S(1)} %copy.38, s32[128,8]{0,1:T(8,128)S(1)} %multiply_add_fusion), kind=kOutput, calls=%fused_computation.60 | convolution fusion | flops 83951616 | bytes 266240 | tf_op jit(solution)/shard_map/aksy,skx->ayx/dot_general | solution.py:100
  337.7 2.2 collective-permute-done
  339.9 3.6 %fusion.86 = bf16[16,512]{1,0:T(8,128)(2,1)} fusion(bf16[4,1024,512]{2,1,0:T(8,128)(2,1)} %gather_fusion, bf16[4,8,1024]{2,1,0:T(8,128)(2,1)S(1)} %get-tuple-element.10, bf16[4,8,1024]{2,1,0:T(8,128)(2,1)S(1)} %get-tuple-element.9, s32[16]{0:T(128)S(1)} %iota_add_fusion, pred[16]{0:T(512)(128)(4,1)S(1)} %iota_compare_fusion.1), kind=kOutput, calls=%fused_computation.64 | convolution fusion | flops 69542912 | bytes 4341840 | tf_op jit(solution)/shard_map/ayx,axp->yp/dot_general | solution.py:110
  (39 shorter events, 11.2 us)
Async XLA Ops:
  6.5 0.9 copy-start
  28.0 37.0 %all-to-all-start.1 = ((bf16[128,2,256]{2,1,0:T(2,128)(2,1)}), bf16[128,2,256]{2,1,0:T(2,128)(2,1)S(1)}, u32[]{:S(2)}, u32[]{:S(2)}) async-start(bf16[128,2,256]{2,1,0:T(2,128)(2,1)} %reshape.156), calls=%async_computation.1 | async-start | bytes 262144 | tf_op jit(solution)/shard_map/all_to_all | solution.py:58
  59.7 4.6 %copy-start.3 = (f32[4]{0:T(128)S(1)}, f32[4]{0:T(128)}, u32[]{:S(2)}) copy-start(f32[4]{0:T(128)} %param.6) | copy-start | bytes 52
  65.0 25.3 %all-to-all-start = ((bf16[128,2,256]{2,1,0:T(2,128)(2,1)}), bf16[128,2,256]{2,1,0:T(2,128)(2,1)S(1)}, u32[]{:S(2)}, u32[]{:S(2)}) async-start(bf16[128,2,256]{2,1,0:T(2,128)(2,1)} %reshape.154), calls=%async_computation | async-start | bytes 262144 | tf_op jit(solution)/shard_map/all_to_all | solution.py:57
  78.8 112.5 %all-reduce.3.cloned.1.call-start = ((), (), s32[]{:S(2)}) async-start(), calls=%async_computation.4 | async-start | bytes 262144 | tf_op jit(solution)/shard_map/psum | solution.py:79
  99.1 16.0 %copy-start.1 = (bf16[8,8,128,8]{3,2,1,0:T(8,128)(2,1)S(1)}, bf16[8,8,128,8]{3,2,1,0:T(8,128)(2,1)}, u32[]{:S(2)}) copy-start(bf16[8,8,128,8]{3,2,1,0:T(8,128)(2,1)} %copy.28) | copy-start | bytes 393220
  131.2 33.4 %copy-start.6 = (s32[1,4]{1,0:T(1,128)S(1)}, s32[1,4]{1,0:T(1,128)}, u32[]{:S(2)}) copy-start(s32[1,4]{1,0:T(1,128)} %param.8) | copy-start | bytes 52
  191.3 16.9 %copy-start.5 = (bf16[4,8,1024]{2,1,0:T(8,128)(2,1)S(1)}, bf16[4,8,1024]{2,1,0:T(8,128)(2,1)}, u32[]{:S(2)}) copy-start(bf16[4,8,1024]{2,1,0:T(8,128)(2,1)} %get-tuple-element.7) | copy-start | bytes 196612
  224.3 32.6 %copy-start.4 = (bf16[4,8,1024]{2,1,0:T(8,128)(2,1)S(1)}, bf16[4,8,1024]{2,1,0:T(8,128)(2,1)}, u32[]{:S(2)}) copy-start(bf16[4,8,1024]{2,1,0:T(8,128)(2,1)} %get-tuple-element.8) | copy-start | bytes 196612
  242.6 32.6 %all-to-all-start.3 = ((bf16[128,2,128]{2,1,0:T(2,128)(2,1)}), bf16[128,2,128]{2,1,0:T(2,128)(2,1)S(1)}, u32[]{:S(2)}, u32[]{:S(2)}) async-start(bf16[128,2,128]{2,1,0:T(2,128)(2,1)} %reshape.160), calls=%async_computation.3 | async-start | bytes 131072 | tf_op jit(solution)/shard_map/all_to_all | solution.py:93
  256.9 32.1 %copy-start.2 = (s32[128]{0:T(128)S(1)}, s32[128]{0:T(128)}, u32[]{:S(2)}) copy-start(s32[128]{0:T(128)} %param.9) | copy-start | bytes 1540
  275.3 25.0 %all-to-all-start.2 = ((bf16[128,2,128]{2,1,0:T(2,128)(2,1)}), bf16[128,2,128]{2,1,0:T(2,128)(2,1)S(1)}, u32[]{:S(2)}, u32[]{:S(2)}) async-start(bf16[128,2,128]{2,1,0:T(2,128)(2,1)} %reshape.158), calls=%async_computation.2 | async-start | bytes 131072 | tf_op jit(solution)/shard_map/all_to_all | solution.py:92
  335.6 4.3 %collective-permute-start = (bf16[4,8,1024]{2,1,0:T(8,128)(2,1)S(1)}, bf16[4,8,1024]{2,1,0:T(8,128)(2,1)S(1)}, u32[]{:S(2)}, u32[]{:S(2)}) collective-permute-start(bf16[4,8,1024]{2,1,0:T(8,128)(2,1)S(1)} %fusion.76), channel_id=1, source_target_pairs={{0,1},{1,0},{2,3},{3,2},{4,5},{5,4},{6,7},{7,6},{8,9},{9,8},{10,11... | collective-permute-start | bytes 196616 | tf_op jit(solution)/shard_map/ppermute | solution.py:15
Sparse Core Ops, SparseCore 0:
  164.7 26.5 all-reduce.2
where the time goes:
time: 357 us; the launch traced here: 351 us
  matrix products  198 us (55%)
  starting transfers between devices  59.2 us (17%)
  local copies, waits for them, and re-layouts  43.4 us (12%)
  waiting for transfers between devices  34.3 us (10%)
  between operations  14.7 us (4%)
    psum x1, waiting for transfers between devices, on_device(): lax.psum(numer_im.astype(jnp.bfloat16), 'dist').astype(jnp.float32)  26.7 us
    unnamed x22, local copies, waits for them, and re-layouts  19.5 us
    dot_general x1, matrix products, on_device(): jnp.einsum('akq,qy->aky', spec_phase_re, sine, preferred_element_type=jnp...  16.9 us
    dot_general x1, matrix products, on_device(): jnp.einsum('aysk,syq->akq', imag_part, col_sin, preferred_element_type=jn...  16.8 us
    dot_general x1, matrix products, on_device(): jnp.einsum('aysk,syq->akq', real_part, col_sin, preferred_element_type=jn...  16.5 us
    dot_general x1, matrix products, on_device(): jnp.dot(flat, sine, preferred_element_type=jnp.float32)  16.1 us
    dot_general x1, matrix products, on_device(): jnp.einsum('akq,qy->aky', spec_phase_im, sine, preferred_element_type=jnp...  16.1 us
    dot_general x1, matrix products, on_device(): jnp.einsum('aysk,syq->akq', real_part, col_cos, preferred_element_type=jn...  16.1 us
  transfers between devices with their start and end apart: 6, of which 4 were waited for; matrix products, arithmetic and copies ran while one was open for 16% of the time, Pallas kernels for 0%

commit v1 on v0

v1 whole, which is shorter than its diff:
```python
import math

import jax
import jax.numpy as jnp
import numpy as np
from jax import lax
from jax.sharding import PartitionSpec as P

absorb_ratio = 0.1
regularizer = 0.05


def cas_table(length):
    index = np.arange(length)
    turned = (index[:, None] * index[None, :] % length) * (2.0 * math.pi / length)
    table = (np.cos(turned) + np.sin(turned)) / math.sqrt(length)
    return jnp.asarray(table.astype(np.float32)).astype(jnp.bfloat16)


def on_device(table, holograms, propagation, weights, angle_order, slab_rows):
    mbatch, angles, dist_dev, rows_dev, width = holograms.shape
    groups = lax.axis_size("rows")
    capacity = 2 * rows_dev
    col_table = table.reshape(groups, rows_dev, width)
    index = jnp.arange(width, dtype=jnp.int32)
    signed = jnp.where(index < width // 2, index, index - width).astype(jnp.float32)
    device = lax.axis_index("rows")
    local_freq = lax.dynamic_slice_in_dim(signed, device * rows_dev, rows_dev, 0)
    radius = (local_freq[:, None] ** 2 + signed[None, :] ** 2) / float(width * width)
    chirp = propagation[:, None, None] * radius[None]
    transfer = 2.0 * (jnp.sin(chirp) + absorb_ratio * jnp.cos(chirp))
    denom = jnp.sum(transfer * transfer, axis=0) + regularizer
    mine = lax.dynamic_slice_in_dim(transfer, lax.axis_index("dist") * dist_dev, dist_dev, 0)
    mine = mine / denom
    parity = device % 2
    offset = parity * slab_rows[device - parity]
    count = slab_rows[device]
    slot = jnp.arange(capacity, dtype=jnp.int32)[:, None]
    source = jnp.arange(capacity, dtype=jnp.int32)[None, :]
    select = ((source == offset + slot) & (slot < count)).astype(jnp.bfloat16)
    flat = holograms[0].reshape(angles * dist_dev * rows_dev, width)
    row = jnp.dot(flat, table, preferred_element_type=jnp.float32).astype(jnp.bfloat16)
    row = row.reshape(angles * dist_dev, rows_dev, width)
    piece = lax.all_to_all(row, "rows", split_axis=2, concat_axis=2, tiled=True)
    piece = piece.reshape(angles * dist_dev, rows_dev, groups, rows_dev)
    spec = jnp.einsum("aysk,syq->akq", piece, col_table, preferred_element_type=jnp.float32)
    spec = spec.reshape(angles, dist_dev, rows_dev, width)
    numer = jnp.sum(mine[None] * spec, axis=1).astype(jnp.bfloat16)
    other = lax.ppermute(numer, "dist", [(0, 1), (1, 0)])
    numer = (numer.astype(jnp.float32) + other.astype(jnp.float32)).astype(jnp.bfloat16)
    half = jnp.einsum("akq,qy->aky", numer, table, preferred_element_type=jnp.float32)
    half = half.astype(jnp.bfloat16)
    piece = lax.all_to_all(half, "rows", split_axis=2, concat_axis=2, tiled=True)
    piece = piece.reshape(angles, rows_dev, groups, rows_dev)
    phase = jnp.einsum("aksy,skx->ayx", piece, col_table, preferred_element_type=jnp.float32)
    phase = phase.astype(jnp.bfloat16)
    chosen = weights[angle_order[0]]
    pairs = [(source, source ^ 1) for source in range(groups)]
    partner = lax.ppermute(phase, "rows", pairs)
    lower = jnp.where(parity == 1, partner, phase)
    upper = jnp.where(parity == 1, phase, partner)
    paired = jnp.concatenate([lower, upper], axis=1)
    rows_in = jnp.einsum("ij,ajx->aix", select, paired, preferred_element_type=jnp.float32)
    rows_in = rows_in.astype(jnp.bfloat16)
    recon = jnp.einsum("ayx,axp->yp", rows_in, chosen, preferred_element_type=jnp.float32)
    return recon.astype(jnp.bfloat16)


def solution(mesh):
    def whole(*args):
        return jax.shard_map(
            on_device,
            mesh=mesh,
            in_specs=(P(), P(None, None, "dist", "rows"), P(), P(None, None, "dist"), P(), P()),
            out_specs=P("rows", "dist"),
            check_vma=False,
        )(cas_table(1024), *args)

    return whole
```

time: 357 us -> 77.3 us (0.22)
  the two profiles are of different devices: /device:TPU:2 before, /device:TPU:1 now
where the time goes in v1:
time: 77.3 us; the launch traced here: 76.7 us
  starting transfers between devices  25.3 us (33%)
  local copies, waits for them, and re-layouts  21.3 us (28%)
  waiting for transfers between devices  17.3 us (22%)
  matrix products  10.5 us (14%)
  other arithmetic  1.42 us (2%)
  between operations  0.89 us (1%)
    all_to_all x1, starting transfers between devices, on_device(): piece = lax.all_to_all(row, 'rows', split_axis=2, concat_axis=2, tiled=True)  16.3 us
    all_to_all x1, waiting for transfers between devices, on_device(): piece = lax.all_to_all(row, 'rows', split_axis=2, concat_axis=2, tiled=True)  10.2 us
    unnamed x14, local copies, waits for them, and re-layouts  9.28 us
    all_to_all x1, starting transfers between devices, on_device(): lax.all_to_all(half, 'rows', split_axis=2, concat_axis=2, tiled=True)  6.28 us
    gather x1, local copies, waits for them, and re-layouts, on_device(): chosen = weights[angle_order[0]]  4.94 us
    dot_general x1, matrix products, on_device(): jnp.einsum('ayx,axp->yp', rows_in, chosen, preferred_element_type=jnp.flo...  3.62 us
    all_to_all x1, waiting for transfers between devices, on_device(): lax.all_to_all(half, 'rows', split_axis=2, concat_axis=2, tiled=True)  3.41 us
    ppermute x1, waiting for transfers between devices, on_device(): partner = lax.ppermute(phase, 'rows', pairs)  2.79 us
  transfers between devices with their start and end apart: 4, of which 4 were waited for; matrix products, arithmetic and copies ran while one was open for 9% of the time, Pallas kernels for 0%

profile of v1, /device:TPU:1, one launch (start us, length us, event | category | flops | bytes accessed | tf_op | source)
XLA Modules:
  0.0 76.7 jit_solution(9320094438461957979)
XLA Ops:
  0.0 0.0 copy-start
  0.0 0.9 %copy-done = bf16[1,4,2,8,1024]{4,3,2,1,0:T(8,128)(2,1)S(1)} copy-done((bf16[1,4,2,8,1024]{4,3,2,1,0:T(8,128)(2,1)S(1)}, bf16[1,4,2,8,1024]{4,3,2,1,0:T(8,128)(2,1)}, u32[]{:S(2)}) %copy-start) | copy-done | bytes 131096
  0.9 2.1 %fusion.4 = bf16[8,8,1024]{2,1,0:T(8,128)(2,1)S(1)} fusion(bf16[64,1024]{1,0:T(8,128)(2,1)S(1)} %bitcast.62, bf16[1024,1024]{1,0:T(8,128)(2,1)} %constant.53.clone), kind=kOutput, calls=%fused_computation.8 | convolution fusion | flops 134283264 | bytes 2359296 | tf_op jit(solution)/shard_map/dot_general | solution.py:42
  3.0 0.0 copy-start.3
  3.0 1.5 %copy.11 = bf16[8,8,1024]{1,0,2:T(8,128)(2,1)S(1)} copy(bf16[8,8,1024]{2,1,0:T(8,128)(2,1)S(1)} %fusion.4) | data formatting | bytes 262144 | tf_op jit(solution)/shard_map/reshape | solution.py:43
  4.5 3.0 %reshape.115 = bf16[128,2,256]{2,1,0:T(2,128)(2,1)} reshape(bf16[1024,8,8]{2,1,0:T(8,128)(2,1)S(1)} %bitcast.63) | data formatting | bytes 262144
  7.5 16.3 %all-to-all-start = ((bf16[128,2,256]{2,1,0:T(2,128)(2,1)}), bf16[128,2,256]{2,1,0:T(2,128)(2,1)S(1)}, u32[]{:S(2)}, u32[]{:S(2)}) async-start(bf16[128,2,256]{2,1,0:T(2,128)(2,1)} %reshape.115), calls=%async_computation | async-start | bytes 262144 | tf_op jit(solution)/shard_map/all_to_all | solution.py:44
  23.9 0.1 dynamic-slice_multiply_fusion
  24.0 0.1 add_multiply_fusion
  24.0 0.0 copy-done.3
  24.0 0.6 multiply_reduce_fusion
  24.6 10.2 %all-to-all-done = bf16[128,2,256]{2,1,0:T(2,128)(2,1)S(1)} async-done(((bf16[128,2,256]{2,1,0:T(2,128)(2,1)}), bf16[128,2,256]{2,1,0:T(2,128)(2,1)S(1)}, u32[]{:S(2)}, u32[]{:S(2)}) %all-to-all-start) | async-done | bytes 131104 | tf_op jit(solution)/shard_map/all_to_all | solution.py:44
  34.8 2.4 %reshape.116 = bf16[1024,8,8]{2,1,0:T(8,128)(2,1)S(1)} reshape(bf16[128,2,256]{2,1,0:T(2,128)(2,1)S(1)} %all-to-all-done) | data formatting | bytes 262144
  37.2 2.2 %copy.13 = bf16[8,8,128,8]{2,1,3,0:T(8,128)(2,1)S(1)} copy(bf16[8,8,128,8]{3,0,1,2:T(8,128)(2,1)S(1)} %bitcast.64) | data formatting | bytes 262144 | tf_op jit(solution)/shard_map/aysk,syq->akq/dot_general | solution.py:46
  39.4 0.0 copy-start.1
  39.4 2.2 %fusion.1 = bf16[4,8,1024]{2,1,0:T(8,128)(2,1)S(1)} fusion(bf16[4,2,8,128,8]{3,2,4,1,0:T(8,128)(2,1)S(1)} %bitcast.67, bf16[128,8,1024,1,1]{2,0,1,4,3:T(8,128)(2,1)} %constant.56, f32[2,8,1024]{2,1,0:T(8,128)S(1)} %dynamic-slice_divide_fusion), kind=kOutput, calls=%fused_computation.3 | convolution fusion | flops 134316032 | bytes 2359296 | tf_op jit(solution)/shard_map/aysk,syq->akq/dot_general | solution.py:46
  41.7 2.2 %collective-permute-start = (bf16[4,8,1024]{2,1,0:T(8,128)(2,1)S(1)}, bf16[4,8,1024]{2,1,0:T(8,128)(2,1)S(1)}, u32[]{:S(2)}, u32[]{:S(2)}) collective-permute-start(bf16[4,8,1024]{2,1,0:T(8,128)(2,1)S(1)} %fusion.1), channel_id=1, source_target_pairs={{0,128},{128,0},{1,129},{129,1},{2,130},{130,2},{3,131},{131,3},{4... | collective-permute-start | bytes 196616 | tf_op jit(solution)/shard_map/ppermute | solution.py:49
  43.9 0.9 %collective-permute-done = bf16[4,8,1024]{2,1,0:T(8,128)(2,1)S(1)} collective-permute-done((bf16[4,8,1024]{2,1,0:T(8,128)(2,1)S(1)}, bf16[4,8,1024]{2,1,0:T(8,128)(2,1)S(1)}, u32[]{:S(2)}, u32[]{:S(2)}) %collective-permute-start) | collective-permute-done | bytes 65568 | tf_op jit(solution)/shard_map/ppermute | solution.py:49
  44.8 0.5 convolution_convert_fusion.2
  45.3 0.7 copy.14
  46.0 1.7 %reshape.117 = bf16[128,2,128]{2,1,0:T(2,128)(2,1)} reshape(bf16[1024,4,8]{2,1,0:T(4,128)(2,1)S(1)} %bitcast.65) | data formatting | bytes 131072
  47.7 6.3 %all-to-all-start.1 = ((bf16[128,2,128]{2,1,0:T(2,128)(2,1)}), bf16[128,2,128]{2,1,0:T(2,128)(2,1)S(1)}, u32[]{:S(2)}, u32[]{:S(2)}) async-start(bf16[128,2,128]{2,1,0:T(2,128)(2,1)} %reshape.117), calls=%async_computation.1 | async-start | bytes 131072 | tf_op jit(solution)/shard_map/all_to_all | solution.py:53
  54.1 0.7 fusion.30
  55.4 4.9 %gather_fusion = bf16[4,1024,512]{2,1,0:T(8,128)(2,1)} fusion(bf16[4,1024,512]{2,1,0:T(8,128)(2,1)} %param.8, s32[1024]{0:T(1024)S(1)} %pad_clamp_fusion), kind=kCustom, calls=%fused_computation | custom fusion | bytes 8388624 | tf_op jit(solution)/shard_map/gather | solution.py:57
  60.3 0.6 iota_compare_fusion.1
  61.0 3.4 %all-to-all-done.1 = bf16[128,2,128]{2,1,0:T(2,128)(2,1)S(1)} async-done(((bf16[128,2,128]{2,1,0:T(2,128)(2,1)}), bf16[128,2,128]{2,1,0:T(2,128)(2,1)S(1)}, u32[]{:S(2)}, u32[]{:S(2)}) %all-to-all-start.1) | async-done | bytes 65568 | tf_op jit(solution)/shard_map/all_to_all | solution.py:53
  64.4 1.2 %reshape.118 = bf16[1024,4,8]{2,1,0:T(4,128)(2,1)S(1)} reshape(bf16[128,2,128]{2,1,0:T(2,128)(2,1)S(1)} %all-to-all-done.1) | data formatting | bytes 131072
  65.6 2.1 %copy.19 = bf16[4,8,128,8]{3,2,1,0:T(8,128)(2,1)S(1)} copy(bf16[4,8,128,8]{1,0,3,2:T(4,128)(2,1)S(1)} %bitcast.66) | data formatting | bytes 131072 | tf_op jit(solution)/shard_map/reshape | solution.py:54
  67.7 2.2 %fusion.5 = bf16[4,8,1024]{2,1,0:T(8,128)(2,1)S(1)} fusion(bf16[4,8,128,8]{3,2,1,0:T(8,128)(2,1)S(1)} %copy.19, bf16[128,8,1024,1]{2,0,1,3:T(8,128)(2,1)} %constant.58), kind=kOutput, calls=%fused_computation.10 | convolution fusion | flops 67141632 | bytes 2228224 | tf_op jit(solution)/shard_map/aksy,skx->ayx/dot_general | solution.py:55
  69.8 0.4 collective-permute-start.1
  70.2 2.8 %collective-permute-done.1 = bf16[4,8,1024]{2,1,0:T(8,128)(2,1)S(1)} collective-permute-done((bf16[4,8,1024]{2,1,0:T(8,128)(2,1)S(1)}, bf16[4,8,1024]{2,1,0:T(8,128)(2,1)S(1)}, u32[]{:S(2)}, u32[]{:S(2)}) %collective-permute-start.1) | collective-permute-done | bytes 65568 | tf_op jit(solution)/shard_map/ppermute | solution.py:59
  73.1 3.6 %fusion.7 = bf16[16,512]{1,0:T(8,128)(2,1)} fusion(bf16[4,1024,512]{2,1,0:T(8,128)(2,1)} %gather_fusion, bf16[4,8,1024]{2,1,0:T(8,128)(2,1)S(1)} %get-tuple-element.6, bf16[4,8,1024]{2,1,0:T(8,128)(2,1)S(1)} %get-tuple-element.5, s32[16]{0:T(128)S(1)} %iota_add_fusion, pred[16]{0:T(512)(128)(4,1)S(1)} %iota_compare_fusion.1), kind=kOutput, calls=%fused_computation.13 | convolution fusion | flops 69542400 | bytes 4341840 | tf_op jit(solution)/shard_map/ayx,axp->yp/dot_general | solution.py:65
  (13 shorter events, 0.1 us)
Async XLA Ops:
  0.0 0.9 %copy-start = (bf16[1,4,2,8,1024]{4,3,2,1,0:T(8,128)(2,1)S(1)}, bf16[1,4,2,8,1024]{4,3,2,1,0:T(8,128)(2,1)}, u32[]{:S(2)}) copy-start(bf16[1,4,2,8,1024]{4,3,2,1,0:T(8,128)(2,1)} %param.6) | copy-start | bytes 393220
  3.0 21.0 %copy-start.3 = (f32[4]{0:T(128)S(1)}, f32[4]{0:T(128)}, u32[]{:S(2)}) copy-start(f32[4]{0:T(128)} %param.7) | copy-start | bytes 52
  7.5 27.3 %all-to-all-start = ((bf16[128,2,256]{2,1,0:T(2,128)(2,1)}), bf16[128,2,256]{2,1,0:T(2,128)(2,1)S(1)}, u32[]{:S(2)}, u32[]{:S(2)}) async-start(bf16[128,2,256]{2,1,0:T(2,128)(2,1)} %reshape.115), calls=%async_computation | async-start | bytes 262144 | tf_op jit(solution)/shard_map/all_to_all | solution.py:44
  39.4 4.5 %copy-start.4 = (s32[1,4]{1,0:T(1,128)S(1)}, s32[1,4]{1,0:T(1,128)}, u32[]{:S(2)}) copy-start(s32[1,4]{1,0:T(1,128)} %param.9) | copy-start | bytes 52
  39.4 5.4 %copy-start.1 = (bf16[1024,1024,1]{1,0,2:T(8,128)(2,1)S(1)}, bf16[1024,1024,1]{1,0,2:T(8,128)(2,1)}, u32[]{:S(2)}) copy-start(bf16[1024,1024,1]{1,0,2:T(8,128)(2,1)} %constant.57) | copy-start | bytes 6291460
  41.7 3.1 %collective-permute-start = (bf16[4,8,1024]{2,1,0:T(8,128)(2,1)S(1)}, bf16[4,8,1024]{2,1,0:T(8,128)(2,1)S(1)}, u32[]{:S(2)}, u32[]{:S(2)}) collective-permute-start(bf16[4,8,1024]{2,1,0:T(8,128)(2,1)S(1)} %fusion.1), channel_id=1, source_target_pairs={{0,128},{128,0},{1,129},{129,1},{2,130},{130,2},{3,131},{131,3},{4... | collective-permute-start | bytes 196616 | tf_op jit(solution)/shard_map/ppermute | solution.py:49
  43.9 10.1 %copy-start.2 = (s32[128]{0:T(128)S(1)}, s32[128]{0:T(128)}, u32[]{:S(2)}) copy-start(s32[128]{0:T(128)} %param.10) | copy-start | bytes 1540
  47.7 16.7 %all-to-all-start.1 = ((bf16[128,2,128]{2,1,0:T(2,128)(2,1)}), bf16[128,2,128]{2,1,0:T(2,128)(2,1)S(1)}, u32[]{:S(2)}, u32[]{:S(2)}) async-start(bf16[128,2,128]{2,1,0:T(2,128)(2,1)} %reshape.117), calls=%async_computation.1 | async-start | bytes 131072 | tf_op jit(solution)/shard_map/all_to_all | solution.py:53
  69.8 3.2 %collective-permute-start.1 = (bf16[4,8,1024]{2,1,0:T(8,128)(2,1)S(1)}, bf16[4,8,1024]{2,1,0:T(8,128)(2,1)S(1)}, u32[]{:S(2)}, u32[]{:S(2)}) collective-permute-start(bf16[4,8,1024]{2,1,0:T(8,128)(2,1)S(1)} %fusion.5), channel_id=1, source_target_pairs={{0,1},{1,0},{2,3},{3,2},{4,5},{5,4},{6,7},{7,6},{8,9},{9,8},{10,11... | collective-permute-start | bytes 196616 | tf_op jit(solution)/shard_map/ppermute | solution.py:59

commit v2 on v1

v2 whole, which is shorter than its diff:
```python
import math

import jax
import jax.numpy as jnp
import numpy as np
from jax import lax
from jax.experimental import pallas as pl
from jax.experimental.pallas import tpu as pltpu
from jax.sharding import PartitionSpec as P

absorb_ratio = 0.1
regularizer = 0.05
MESH = pl.DeviceIdType.MESH
N = 1024
ROWS = 128
ROOT = 1.0 / 32.0
RADIX = 8


def tables():
    long = np.arange(ROWS)
    short = np.arange(RADIX)
    turn = 2.0 * math.pi
    beta = turn * (np.outer(long, long) % ROWS) / ROWS
    cas = [np.cos(beta) + np.sin(beta), np.cos(beta) - np.sin(beta)]
    eye2 = np.eye(2)
    ts, tf, ti = [], [], []
    for c in cas:
        ts.append(np.einsum("tk,bc->tbck", c, eye2).reshape(256, 256))
        tf.append(ts[-1].T)
        ti.append(np.einsum("jpk,bc->pjbck", c.reshape(64, 2, ROWS), eye2).reshape(256, 256))
    phi = turn * (np.outer(short, short) % RADIX) / RADIX
    wave = [np.cos(phi), np.sin(phi)]
    kr = np.concatenate([np.kron(np.eye(16), w) for w in wave], axis=0)
    ki = np.stack([np.einsum("ij,ab,d,my->iadmjby", np.eye(4), np.eye(4), np.ones(2), w) for w in wave])
    ki = np.moveaxis(ki, 0, 4).reshape(256, 256)
    kf = [
        np.einsum("ibx,ac,yz->biayxcz", w.reshape(4, 2, RADIX), np.eye(4), np.eye(8))
        for w in wave
    ]
    kf = np.stack(kf).reshape(512, 256)
    theta = turn * np.outer(short, long) / N
    rowtab = np.concatenate([np.cos(theta), np.sin(theta)], axis=0) * ROOT
    lanes = np.arange(128)
    tk = theta.T[:, lanes % RADIX]
    coltab = np.concatenate([np.cos(tk), np.sin(tk)], axis=0) * ROOT
    tx = np.concatenate([theta.T[:, 2 * (lanes // 32) + b] for b in range(2)], axis=0)
    outtab = np.concatenate([np.cos(tx), np.sin(tx)], axis=0) * ROOT
    first = np.concatenate(ts, axis=1)
    rest = np.concatenate(tf + ti + [ki, kf, np.pad(kr, ((0, 0), (0, 128)))], axis=0)
    half = lambda v: np.asarray(v, np.float32).astype(jnp.bfloat16)
    wide = np.concatenate([coltab, outtab], axis=0)
    return half(first), rowtab.astype(np.float32), half(rest), wide.astype(np.float32)


def dot(a, b):
    return jnp.dot(a, b, preferred_element_type=jnp.float32)


def half(value):
    return value.astype(jnp.bfloat16)


def row_stage(holo, first, rowtab):
    h = [holo[:, 128 * i : 128 * (i + 1)].astype(jnp.float32) for i in range(RADIX)]
    e = [h[i] + h[i + 4] for i in range(4)]
    o = [h[i] - h[i + 4] for i in range(4)]
    c = math.sqrt(0.5)
    even, odd = e[0] + e[2], e[1] + e[3]
    minus, plus = c * (o[1] - o[3]), c * (o[1] + o[3])
    p0, p4 = even + odd, even - odd
    p2, q2 = e[0] - e[2], e[1] - e[3]
    p1, q1 = o[0] + minus, o[2] + plus
    p3, q3 = o[0] - minus, plus - o[2]
    parts = [(p0, None), (p1, q1), (p2, q2), (p3, q3), (p4, None), (p3, -q3), (p2, -q2), (p1, -q1)]
    straight, turned = [], []
    for j, (p, q) in enumerate(parts):
        cos, sin = rowtab[j : j + 1, :], rowtab[RADIX + j : RADIX + j + 1, :]
        if q is None:
            straight.append(half(cos * p))
            turned.append(half(sin * p))
        else:
            straight.append(half(cos * p - sin * q))
            turned.append(half(sin * p + cos * q))
    blocks = [
        jnp.concatenate([straight[2 * i], straight[2 * i + 1], turned[2 * i], turned[2 * i + 1]], axis=1)
        for i in range(4)
    ]
    rhs = jnp.concatenate(blocks, axis=0)
    out = lax.dot_general(first, rhs, (((1,), (1,)), ((), ())), preferred_element_type=jnp.float32)
    return half(out)


def sine(x):
    n = jnp.floor(x * (1.0 / math.pi) + 0.5)
    r = x - n * 3.140625
    r = r - n * 9.67502593994140625e-4
    r = r - n * 1.509957990978376432e-7
    s = r * r
    w = -2.5052108385441718775e-8
    for coefficient in (
        2.7557319223985890653e-6,
        -1.9841269841269841253e-4,
        8.3333333333333332177e-3,
        -1.6666666666666665741e-1,
    ):
        w = w * s + coefficient
    value = r + r * s * w
    return jnp.where(n - 2.0 * jnp.floor(n * 0.5) > 0.5, -value, value)


def roll(value, shift):
    return pltpu.roll(value, shift % 128, 1)


def filter_stage(dist, me, speeds, roll=roll):
    lane = lax.broadcasted_iota(jnp.int32, (1, 128), 1)
    m = lane % 8
    second = (lane // 8) % 2 == 1
    odd_angle = (lane // 16) % 2 == 1
    other = odd_angle != (dist == 1)
    speed = jnp.where(
        other,
        jnp.where(second, speeds[3], speeds[2]),
        jnp.where(second, speeds[1], speeds[0]),
    )
    k = lax.broadcasted_iota(jnp.int32, (128, 128), 0)
    ky = k + 128 * m
    ky = jnp.where(ky < 512, ky, ky - 1024).astype(jnp.float32)
    ky2 = ky * ky
    shift = math.atan(absorb_ratio)
    gain = 2.0 * math.sqrt(1.0 + absorb_ratio * absorb_ratio)
    result = []
    for g in range(2):
        blocks = []
        for b in range(2):
            kx = 8 * me + 4 * g + 2 * (lane // 64) + b
            kx = jnp.where(kx < 512, kx, kx - 1024).astype(jnp.float32)
            radius = (ky2 + kx * kx) * (1.0 / (N * N))
            t = gain * sine(speed * radius + shift)
            total = t * t
            total = total + jnp.where(second, roll(total, 8), roll(total, -8))
            total = total + jnp.where(odd_angle, roll(total, 16), roll(total, -16))
            f = t / (total + regularizer)
            blocks.append(jnp.where(odd_angle, roll(f, 16), f))
        result.append(jnp.concatenate(blocks, axis=0))
    return result


def twist(cos, sin, u, v):
    return cos * u + sin * v, cos * v - sin * u


def twice(table):
    return jnp.concatenate([table, table], axis=0)


def column_stage(groups, tf0, tf1, kr, ki, ti0, ti1, coltab, filters):
    cos, sin = twice(coltab[0:128]), twice(coltab[128:256])
    r = jnp.concatenate(groups, axis=1)
    u, v = dot(tf0, r), dot(tf1, r)
    numer = []
    for g in range(2):
        part = slice(128 * g, 128 * g + 128)
        x, y = twist(cos, sin, u[:, part], v[:, part])
        spec = dot(jnp.concatenate([half(x), half(y)], axis=1), kr)
        numer.append(half(spec * filters[g]))
    pq = dot(jnp.concatenate(numer, axis=1), ki)
    p, q = pq[:, 0:128], pq[:, 128:256]
    straight = half(cos * p - sin * q)
    turned = half(sin * p + cos * q)
    return half(dot(ti0, straight) + dot(ti1, turned))


def last_stage(pair, tf0, tf1, kf, outtab):
    cos, sin = outtab[0:256], outtab[256:512]
    r = jnp.concatenate(pair, axis=1)
    u, v = dot(tf0, r), dot(tf1, r)
    rows = []
    for p in range(2):
        part = slice(128 * p, 128 * p + 128)
        x, y = twist(cos, sin, u[:, part], v[:, part])
        x, y = half(x), half(y)
        rows.append(jnp.concatenate([x[0:128], x[128:256], y[0:128], y[128:256]], axis=1))
    return dot(jnp.concatenate(rows, axis=0), kf)


def recon_stage(phase, weight_of):
    turned = [
        [phase[128 * p : 128 * p + 128, 128 * g : 128 * g + 128].T for g in range(2)] for p in range(2)
    ]
    total = None
    for a in range(4):
        tiles = []
        for xm in range(RADIX):
            g, at = xm // 4, ((xm % 4) * 4 + a) * 8
            tiles.append(jnp.concatenate([turned[p][g][at : at + 8] for p in range(2)], axis=0))
        lhs = half(jnp.concatenate(tiles, axis=1))
        term = dot(lhs, weight_of(a))
        total = term if total is None else total + term
    return total


def kernel(
    holo_hbm, speed_ref, weights_hbm, order_ref, slab_ref, first_hbm, rowtab_hbm, rest_hbm, wide_hbm,
    out_ref,
    holo, weights, first, rowtab, rest, wide, m1, r1, m2, r2, e1, e2, junk1, junk2,
    load_sem, weight_sem, send_sem, recv_sem,
):
    dist = lax.axis_index("dist")
    me = lax.axis_index("rows")
    barrier = pltpu.get_barrier_semaphore()

    def greet(t, carry):
        pl.semaphore_signal(barrier, inc=1, device_id=(dist, t), device_id_type=MESH)
        return carry

    lax.fori_loop(me + 1, ROWS, greet, 0)
    lax.fori_loop(0, me, greet, 0)
    pl.semaphore_signal(barrier, inc=1, device_id=(1 - dist, me), device_id_type=MESH)

    loads = [
        pltpu.make_async_copy(source, target, load_sem.at[i])
        for i, (source, target) in enumerate(
            [(holo_hbm, holo), (first_hbm, first), (rowtab_hbm, rowtab), (rest_hbm, rest), (wide_hbm, wide)]
        )
    ]
    for load in loads:
        load.start()
    big = pltpu.make_async_copy(weights_hbm, weights, weight_sem)
    big.start()
    for load in loads[:3]:
        load.wait()
    spectrum = row_stage(holo[...], first[...], rowtab[...])
    m1[0] = spectrum[:, 0:128]
    m1[1] = spectrum[:, 128:256]
    pl.semaphore_wait(barrier, ROWS)

    def send_all(source, sources, target, junk, index):
        mine = target.at[:, pl.ds(pl.multiple_of(2 * me, 2), 2), :]

        def send(t, carry):
            pltpu.make_async_remote_copy(
                src_ref=source(t),
                dst_ref=mine,
                send_sem=send_sem.at[index],
                recv_sem=recv_sem.at[index],
                device_id=(dist, t),
                device_id_type=MESH,
            ).start()
            return carry

        lax.fori_loop(me + 1, ROWS, send, 0)
        lax.fori_loop(0, me, send, 0)
        pltpu.make_async_copy(source(me), mine, recv_sem.at[index]).start()
        pltpu.make_async_copy(source(me), junk, send_sem.at[index]).start()

    send_all(lambda t: m1.at[:, pl.ds(pl.multiple_of(2 * t, 2), 2), :], m1, r1, junk1, 0)
    for load in loads[3:]:
        load.wait()
    speeds = [speed_ref[i] for i in range(4)]
    filters = filter_stage(dist, me, speeds)
    tf0, tf1, ti0, ti1 = (rest[256 * i : 256 * i + 256, :] for i in range(4))
    ki, kf, kr = rest[1024:1280, :], rest[1280:1792, :], rest[1792:2048, 0:128]
    coltab, outtab = wide[0:256, :], wide[256:768, :]
    pltpu.make_async_copy(r1, r1, recv_sem.at[0]).wait()
    inverse = column_stage([r1[0], r1[1]], tf0, tf1, kr, ki, ti0, ti1, coltab, filters)
    m2[0] = inverse[0:128]
    m2[1] = inverse[128:256]
    send_all(lambda t: m2.at[:, pl.ds(pl.multiple_of(2 * (t // 2), 2), 2), :], m2, r2, junk2, 1)
    big.wait()
    pltpu.make_async_copy(r2, r2, recv_sem.at[1]).wait()
    partial = last_stage([r2[0], r2[1]], tf0, tf1, kf, outtab)
    e1[...] = half(partial)
    swap = pltpu.make_async_remote_copy(
        src_ref=e1,
        dst_ref=e2,
        send_sem=send_sem.at[2],
        recv_sem=recv_sem.at[2],
        device_id=(1 - dist, me),
        device_id_type=MESH,
    )
    swap.start()
    swap.wait_recv()
    phase = partial + e2[...].astype(jnp.float32)
    recon = half(recon_stage(phase, lambda a: weights[order_ref[0, a]]))
    parity = me % 2
    offset = parity * slab_ref[me - parity]
    count = slab_ref[me]
    slot = lax.broadcasted_iota(jnp.int32, (16, 16), 0)
    source = lax.broadcasted_iota(jnp.int32, (16, 16), 1)
    select = half(((source == offset + slot) & (slot < count)).astype(jnp.float32))
    out_ref[...] = half(dot(select, recon))
    swap.wait_send()
    pltpu.make_async_copy(m1, m1, send_sem.at[0]).wait()
    pltpu.make_async_copy(r2, r2, send_sem.at[1]).wait()


def on_device(first, rowtab, rest, wide, holograms, propagation, weights, angle_order, slab_rows):
    pixels = weights.shape[2]
    holo = holograms.reshape(64, N)
    anywhere = pl.BlockSpec(memory_space=pl.ANY)
    scalar = pl.BlockSpec(memory_space=pltpu.SMEM)
    vmem = pltpu.VMEM
    lo = jnp.bfloat16
    return pl.pallas_call(
        kernel,
        out_shape=jax.ShapeDtypeStruct((16, pixels), lo),
        in_specs=[anywhere, scalar, anywhere, scalar, scalar] + [anywhere] * 4,
        out_specs=pl.BlockSpec(memory_space=vmem),
        scratch_shapes=[
            vmem(holo.shape, lo),
            vmem(weights.shape, lo),
            vmem(first.shape, lo),
            vmem(rowtab.shape, jnp.float32),
            vmem(rest.shape, lo),
            vmem(wide.shape, jnp.float32),
            vmem((2, 256, 128), lo),
            vmem((2, 256, 128), lo),
            vmem((2, 128, 128), lo),
            vmem((2, 256, 128), lo),
            vmem((256, 256), lo),
            vmem((256, 256), lo),
            vmem((2, 2, 128), lo),
            vmem((2, 2, 128), lo),
            pltpu.SemaphoreType.DMA((5,)),
            pltpu.SemaphoreType.DMA,
            pltpu.SemaphoreType.DMA((3,)),
            pltpu.SemaphoreType.DMA((3,)),
        ],
        compiler_params=pltpu.CompilerParams(collective_id=0, has_side_effects=True),
    )(holo, propagation, weights, angle_order, slab_rows, first, rowtab, rest, wide)


def solution(mesh):
    constants = tables()

    def whole(*args):
        return jax.shard_map(
            on_device,
            mesh=mesh,
            in_specs=(P(),) * 4
            + (P(None, None, "dist", "rows"), P(), P(None, None, "dist"), P(), P()),
            out_specs=P("rows", "dist"),
            check_vma=False,
        )(*(jnp.asarray(c) for c in constants), *args)

    return whole
```

time: 77.3 us -> 36 us (0.47)
  Pallas kernels: 0 us -> 34.5 us
  starting transfers between devices: 25.3 us -> 0 us
  local copies, waits for them, and re-layouts: 21.3 us -> 1.32 us
  waiting for transfers between devices: 17.3 us -> 0 us
  matrix products: 10.5 us -> 0 us
  other arithmetic: 1.42 us -> 0 us
  between operations: 0.89 us -> 0.01 us
    pallas_call x0 -> x1, Pallas kernels: none -> 34.5 us  [on_device(): pl.pallas_call(kernel, out_shape=jax.ShapeDtypeStruct((16, pixels), lo),...]
    all_to_all x2 -> x0, starting transfers between devices: 22.6 us -> none  [the longest x1 16.3 us: on_device(): piece = lax.all_to_all(row, 'rows', split_axis=2, concat_axis=2, tiled=True)]
    all_to_all x2 -> x0, waiting for transfers between devices: 13.6 us -> none  [the longest x1 10.2 us: on_device(): piece = lax.all_to_all(row, 'rows', split_axis=2, concat_axis=2, tiled=True)]
    dot_general x5 -> x0, matrix products: 10.5 us -> none  [the longest x1 3.62 us: on_device(): jnp.einsum('ayx,axp->yp', rows_in, chosen, preferred_element_type=jnp.flo...]
    unnamed x14 -> x1, local copies, waits for them, and re-layouts: 9.28 us -> 1.32 us
    gather x1 -> x0, local copies, waits for them, and re-layouts: 4.94 us -> none  [on_device(): chosen = weights[angle_order[0]]]
    ppermute x2 -> x0, waiting for transfers between devices: 3.69 us -> none  [the longest x1 2.79 us: on_device(): partner = lax.ppermute(phase, 'rows', pairs)]
    reshape x2 -> x0, local copies, waits for them, and re-layouts: 3.57 us -> none  [the longest x1 2.06 us: on_device(): piece = piece.reshape(angles, rows_dev, groups, rows_dev)]
  transfers between devices with their start and end apart: 4 -> 0, of which waited for: 4 -> 0; matrix products, arithmetic and copies ran while one was open for 9% -> 0% of each run, Pallas kernels for 0% -> 0%
where the time goes in v2:
time: 36 us; the launch traced here: 35.8 us
  Pallas kernels  34.5 us (96%)
  local copies, waits for them, and re-layouts  1.32 us (4%)
    pallas_call x1, Pallas kernels, on_device(): pl.pallas_call(kernel, out_shape=jax.ShapeDtypeStruct((16, pixels), lo),...  34.5 us
    unnamed x1, local copies, waits for them, and re-layouts  1.32 us

profile of v2, /device:TPU:1, one launch (start us, length us, event | category | flops | bytes accessed | tf_op | source)
XLA Modules:
  0.0 35.8 jit_solution(18034804180649755184)
XLA Ops:
  0.0 34.5 %shard_map.91 = bf16[16,512]{1,0:T(8,128)(2,1)} custom-call(bf16[64,1024]{1,0:T(8,128)(2,1)} %bitcast.1, f32[4]{0:T(128)} %speed_ref.1, bf16[4,1024,512]{2,1,0:T(8,128)(2,1)} %weights_hbm.1, s32[1,4]{1,0:T(1,128)} %order_ref.1, s32[128]{0:T(128)} %slab_ref.1, bf16[256,512]{1,0:T(8,128)(2,1)} %constant.8.clone.first_hbm, f32[16,128]{1,0:T(8,128)} %constant.9.clone.rowtab_hbm, ...), custom_call_target="tpu_custom_call" | custom-call | tf_op jit(solution)/shard_map/pallas_call | solution.py:306
  34.5 1.3 %copy.11 = bf16[16,512]{1,0:T(8,128)(2,1)} copy(bf16[16,512]{1,0:T(8,128)(2,1)} %shard_map.91) | data formatting | bytes 32768

commit v3 on v2

--- a/solution.py
+++ b/solution.py
@@ -169,7 +169,7 @@
     p, q = pq[:, 0:128], pq[:, 128:256]
     straight = half(cos * p - sin * q)
     turned = half(sin * p + cos * q)
-    return half(dot(ti0, straight) + dot(ti1, turned))
+    return dot(ti0, straight) + dot(ti1, turned)
 
 
 def last_stage(pair, tf0, tf1, kf, outtab):
@@ -201,28 +201,50 @@
     return total
 
 
+def far_first(me, act):
+    y, z, x = me // 32, (me // 4) % 8, me % 4
+    ys = [(y + i) % 4 * 32 for i in range(4)]
+    xs = [(x + i) % 4 for i in range(4)]
+    away = [0, 1, 2, 1]
+    plane = sorted(((i, j) for i in range(4) for j in range(4)), key=lambda p: -away[p[0]] - away[p[1]])
+    bases = {p: ys[p[0]] + xs[p[1]] for p in plane}
+
+    def layer(step, carry):
+        hop = (step + 1) // 2
+        at = (z + 4 + hop * (1 - 2 * (step % 2)) + 8) % 8 * 4
+        for p in plane[:-1]:
+            act(bases[p] + at)
+
+        @pl.when(step < 7)
+        def _():
+            act(bases[plane[-1]] + at)
+
+        return carry
+
+    lax.fori_loop(0, 8, layer, 0)
+
+
 def kernel(
-    holo_hbm, speed_ref, weights_hbm, order_ref, slab_ref, first_hbm, rowtab_hbm, rest_hbm, wide_hbm,
+    holo_hbm, speed_hbm, weights_hbm, order_hbm, slab_hbm, first_hbm, rowtab_hbm, rest_hbm, wide_hbm,
     out_ref,
-    holo, weights, first, rowtab, rest, wide, m1, r1, m2, r2, e1, e2, junk1, junk2,
+    holo, weights, first, rowtab, rest, wide, m1, r1, m2, r2, e1, e2, junk1, junk2, speed_ref, order_ref, slab_ref,
     load_sem, weight_sem, send_sem, recv_sem,
 ):
     dist = lax.axis_index("dist")
     me = lax.axis_index("rows")
     barrier = pltpu.get_barrier_semaphore()
 
-    def greet(t, carry):
+    def greet(t):
         pl.semaphore_signal(barrier, inc=1, device_id=(dist, t), device_id_type=MESH)
-        return carry
-
-    lax.fori_loop(me + 1, ROWS, greet, 0)
-    lax.fori_loop(0, me, greet, 0)
+
+    far_first(me, greet)
     pl.semaphore_signal(barrier, inc=1, device_id=(1 - dist, me), device_id_type=MESH)
 
     loads = [
         pltpu.make_async_copy(source, target, load_sem.at[i])
         for i, (source, target) in enumerate(
-            [(holo_hbm, holo), (first_hbm, first), (rowtab_hbm, rowtab), (rest_hbm, rest), (wide_hbm, wide)]
+            [(holo_hbm, holo), (first_hbm, first), (rowtab_hbm, rowtab), (rest_hbm, rest), (wide_hbm, wide),
+             (speed_hbm, speed_ref), (order_hbm, order_ref), (slab_hbm, slab_ref)]
         )
     ]
     for load in loads:
@@ -239,7 +261,7 @@
     def send_all(source, sources, target, junk, index):
         mine = target.at[:, pl.ds(pl.multiple_of(2 * me, 2), 2), :]
 
-        def send(t, carry):
+        def send(t):
             pltpu.make_async_remote_copy(
                 src_ref=source(t),
                 dst_ref=mine,
@@ -248,10 +270,8 @@
                 device_id=(dist, t),
                 device_id_type=MESH,
             ).start()
-            return carry
-
-        lax.fori_loop(me + 1, ROWS, send, 0)
-        lax.fori_loop(0, me, send, 0)
+
+        far_first(me, send)
         pltpu.make_async_copy(source(me), mine, recv_sem.at[index]).start()
         pltpu.make_async_copy(source(me), junk, send_sem.at[index]).start()
 
@@ -265,13 +285,7 @@
     coltab, outtab = wide[0:256, :], wide[256:768, :]
     pltpu.make_async_copy(r1, r1, recv_sem.at[0]).wait()
     inverse = column_stage([r1[0], r1[1]], tf0, tf1, kr, ki, ti0, ti1, coltab, filters)
-    m2[0] = inverse[0:128]
-    m2[1] = inverse[128:256]
-    send_all(lambda t: m2.at[:, pl.ds(pl.multiple_of(2 * (t // 2), 2), 2), :], m2, r2, junk2, 1)
-    big.wait()
-    pltpu.make_async_copy(r2, r2, recv_sem.at[1]).wait()
-    partial = last_stage([r2[0], r2[1]], tf0, tf1, kf, outtab)
-    e1[...] = half(partial)
+    e1[...] = half(inverse)
     swap = pltpu.make_async_remote_copy(
         src_ref=e1,
         dst_ref=e2,
@@ -282,7 +296,13 @@
     )
     swap.start()
     swap.wait_recv()
-    phase = partial + e2[...].astype(jnp.float32)
+    inverse = half(inverse + e2[...].astype(jnp.float32))
+    m2[0] = inverse[0:128]
+    m2[1] = inverse[128:256]
+    send_all(lambda t: m2.at[:, pl.ds(pl.multiple_of(2 * (t // 2), 2), 2), :], m2, r2, junk2, 1)
+    big.wait()
+    pltpu.make_async_copy(r2, r2, recv_sem.at[1]).wait()
+    phase = last_stage([r2[0], r2[1]], tf0, tf1, kf, outtab)
     recon = half(recon_stage(phase, lambda a: weights[order_ref[0, a]]))
     parity = me % 2
     offset = parity * slab_ref[me - parity]
@@ -300,13 +320,12 @@
     pixels = weights.shape[2]
     holo = holograms.reshape(64, N)
     anywhere = pl.BlockSpec(memory_space=pl.ANY)
-    scalar = pl.BlockSpec(memory_space=pltpu.SMEM)
     vmem = pltpu.VMEM
     lo = jnp.bfloat16
     return pl.pallas_call(
         kernel,
-        out_shape=jax.ShapeDtypeStruct((16, pixels), lo),
-        in_specs=[anywhere, scalar, anywhere, scalar, scalar] + [anywhere] * 4,
+        out_shape=pltpu.VMEM((16, pixels), lo),
+        in_specs=[anywhere] * 9,
         out_specs=pl.BlockSpec(memory_space=vmem),
         scratch_shapes=[
             vmem(holo.shape, lo),
@@ -319,11 +338,14 @@
             vmem((2, 256, 128), lo),
             vmem((2, 128, 128), lo),
             vmem((2, 256, 128), lo),
-            vmem((256, 256), lo),
-            vmem((256, 256), lo),
+            vmem((256, 128), lo),
+            vmem((256, 128), lo),
             vmem((2, 2, 128), lo),
             vmem((2, 2, 128), lo),
-            pltpu.SemaphoreType.DMA((5,)),
+            pltpu.SMEM(propagation.shape, jnp.float32),
+            pltpu.SMEM(angle_order.shape, jnp.int32),
+            pltpu.SMEM(slab_rows.shape, jnp.int32),
+            pltpu.SemaphoreType.DMA((8,)),
             pltpu.SemaphoreType.DMA,
             pltpu.SemaphoreType.DMA((3,)),
             pltpu.SemaphoreType.DMA((3,)),

time: 36 us -> 31.7 us (0.88)
  Pallas kernels: 34.5 us -> 31 us
  local copies, waits for them, and re-layouts: 1.32 us -> 0.61 us
    pallas_call x1, Pallas kernels: 34.5 us -> 31 us  [on_device(): pl.pallas_call(kernel, out_shape=pltpu.VMEM((16, pixels), lo), in_specs=[...]
    unnamed x1, local copies, waits for them, and re-layouts: 1.32 us -> 0.61 us
where the time goes in v3:
time: 31.7 us; the launch traced here: 31.6 us
  Pallas kernels  31 us (98%)
  local copies, waits for them, and re-layouts  0.61 us (2%)
    pallas_call x1, Pallas kernels, on_device(): pl.pallas_call(kernel, out_shape=pltpu.VMEM((16, pixels), lo), in_specs=[...  31 us

profile of v3, /device:TPU:1, one launch (start us, length us, event | category | flops | bytes accessed | tf_op | source)
XLA Modules:
  0.0 31.6 jit_solution(5359168301164964381)
XLA Ops:
  0.0 31.0 %shard_map.91 = bf16[16,512]{1,0:T(8,128)(2,1)S(1)} custom-call(bf16[64,1024]{1,0:T(8,128)(2,1)} %bitcast.1, f32[4]{0:T(128)} %speed_hbm.1, bf16[4,1024,512]{2,1,0:T(8,128)(2,1)} %weights_hbm.1, s32[1,4]{1,0:T(1,128)} %order_hbm.1, s32[128]{0:T(128)} %slab_hbm.1, bf16[256,512]{1,0:T(8,128)(2,1)} %constant.8.clone.first_hbm, ...), custom_call_target="tpu_custom_call" | custom-call | tf_op jit(solution)/shard_map/pallas_call | solution.py:325
  31.0 0.6 %copy.11 = bf16[16,512]{1,0:T(8,128)(2,1)} copy(bf16[16,512]{1,0:T(8,128)(2,1)S(1)} %shard_map.91) | data formatting | bytes 32768

commit v4 on v3

--- a/solution.py
+++ b/solution.py
@@ -25,8 +25,9 @@
     cas = [np.cos(beta) + np.sin(beta), np.cos(beta) - np.sin(beta)]
     eye2 = np.eye(2)
     ts, tf, ti = [], [], []
+    place = long.reshape(4, 8, 4).transpose(1, 0, 2).reshape(-1)
     for c in cas:
-        ts.append(np.einsum("tk,bc->tbck", c, eye2).reshape(256, 256))
+        ts.append(np.einsum("tk,bc->tbck", c[place], eye2).reshape(256, 256))
         tf.append(ts[-1].T)
         ti.append(np.einsum("jpk,bc->pjbck", c.reshape(64, 2, ROWS), eye2).reshape(256, 256))
     phi = turn * (np.outer(short, short) % RADIX) / RADIX
@@ -201,23 +202,30 @@
     return total
 
 
+HOPS = [0, 1, 2, 1]
+PLANE = sorted(((i, j) for i in range(4) for j in range(4)), key=lambda p: -HOPS[p[0]] - HOPS[p[1]])[:-1]
+LINE = [4, 3, 5, 2, 6, 1, 7]
+
+
+def spot(me):
+    return me // 32, (me // 4) % 8, me % 4
+
+
 def far_first(me, act):
-    y, z, x = me // 32, (me // 4) % 8, me % 4
+    y, z, x = spot(me)
     ys = [(y + i) % 4 * 32 for i in range(4)]
     xs = [(x + i) % 4 for i in range(4)]
-    away = [0, 1, 2, 1]
-    plane = sorted(((i, j) for i in range(4) for j in range(4)), key=lambda p: -away[p[0]] - away[p[1]])
-    bases = {p: ys[p[0]] + xs[p[1]] for p in plane}
+    bases = {p: ys[p[0]] + xs[p[1]] for p in PLANE}
 
     def layer(step, carry):
         hop = (step + 1) // 2
         at = (z + 4 + hop * (1 - 2 * (step % 2)) + 8) % 8 * 4
-        for p in plane[:-1]:
+        for p in PLANE:
             act(bases[p] + at)
 
         @pl.when(step < 7)
         def _():
-            act(bases[plane[-1]] + at)
+            act(ys[0] + xs[0] + at)
 
         return carry
 
@@ -227,7 +235,7 @@
 def kernel(
     holo_hbm, speed_hbm, weights_hbm, order_hbm, slab_hbm, first_hbm, rowtab_hbm, rest_hbm, wide_hbm,
     out_ref,
-    holo, weights, first, rowtab, rest, wide, m1, r1, m2, r2, e1, e2, junk1, junk2, speed_ref, order_ref, slab_ref,
+    holo, weights, first, rowtab, rest, wide, m1, b1, r1, m2, r2, e1, e2, junk, speed_ref, order_ref, slab_ref,
     load_sem, weight_sem, send_sem, recv_sem,
 ):
     dist = lax.axis_index("dist")
@@ -236,9 +244,6 @@
 
     def greet(t):
         pl.semaphore_signal(barrier, inc=1, device_id=(dist, t), device_id_type=MESH)
-
-    far_first(me, greet)
-    pl.semaphore_signal(barrier, inc=1, device_id=(1 - dist, me), device_id_type=MESH)
 
     loads = [
         pltpu.make_async_copy(source, target, load_sem.at[i])
@@ -247,35 +252,61 @@
              (speed_hbm, speed_ref), (order_hbm, order_ref), (slab_hbm, slab_ref)]
         )
     ]
-    for load in loads:
+    for load in loads[:3]:
+        load.start()
+    y, z, x = spot(me)
+    line = [(z + i) % 8 for i in LINE]
+    plane = [((y + i) % 4, (x + j) % 4) for i, j in PLANE]
+    for at in line:
+        greet(y * 32 + at * 4 + x)
+    for at, to in plane:
+        greet(at * 32 + z * 4 + to)
+    pl.semaphore_signal(barrier, inc=1, device_id=(1 - dist, me), device_id_type=MESH)
+    for load in loads[3:]:
         load.start()
     big = pltpu.make_async_copy(weights_hbm, weights, weight_sem)
     big.start()
     for load in loads[:3]:
         load.wait()
     spectrum = row_stage(holo[...], first[...], rowtab[...])
-    m1[0] = spectrum[:, 0:128]
-    m1[1] = spectrum[:, 128:256]
-    pl.semaphore_wait(barrier, ROWS)
-
-    def send_all(source, sources, target, junk, index):
-        mine = target.at[:, pl.ds(pl.multiple_of(2 * me, 2), 2), :]
-
-        def send(t):
-            pltpu.make_async_remote_copy(
-                src_ref=source(t),
-                dst_ref=mine,
-                send_sem=send_sem.at[index],
-                recv_sem=recv_sem.at[index],
-                device_id=(dist, t),
-                device_id_type=MESH,
-            ).start()
-
-        far_first(me, send)
-        pltpu.make_async_copy(source(me), mine, recv_sem.at[index]).start()
-        pltpu.make_async_copy(source(me), junk, send_sem.at[index]).start()
-
-    send_all(lambda t: m1.at[:, pl.ds(pl.multiple_of(2 * t, 2), 2), :], m1, r1, junk1, 0)
+    for i in range(8):
+        for g in range(2):
+            m1[2 * i + g] = spectrum[32 * i : 32 * i + 32, 128 * g : 128 * g + 128]
+    pl.semaphore_wait(barrier, len(LINE) + len(PLANE) + 1)
+
+    def push(source, target, sent, landed, peer):
+        pltpu.make_async_remote_copy(
+            src_ref=source,
+            dst_ref=target,
+            send_sem=send_sem.at[sent],
+            recv_sem=recv_sem.at[landed],
+            device_id=(dist, peer),
+            device_id_type=MESH,
+        ).start()
+
+    def along_line(source, target, landed):
+        mine = target.at[pl.ds(2 * z, 2)]
+        for at in line:
+            push(source.at[pl.ds(2 * at, 2)], mine, 0, landed, y * 32 + at * 4 + x)
+        pltpu.make_async_copy(source.at[pl.ds(2 * z, 2)], mine, recv_sem.at[landed]).start()
+
+    def in_plane(source, target, landed):
+        def column(at, to):
+            return pl.ds(pl.multiple_of(8 * at + 2 * to, 2), 2)
+
+        mine = target.at[:, column(y, x), :]
+        for at, to in plane:
+            push(source.at[:, column(at, to), :], mine, 2, landed, at * 32 + z * 4 + to)
+        pltpu.make_async_copy(source.at[:, column(y, x), :], mine, recv_sem.at[landed]).start()
+
+    for core, steps in enumerate([(along_line, in_plane), (in_plane, along_line)]):
+
+        @pl.when(dist == core)
+        def _():
+            steps[0](m1, b1, 0)
+            pltpu.make_async_copy(b1, b1, recv_sem.at[0]).wait()
+            steps[1](b1, r1, 1)
+
     for load in loads[3:]:
         load.wait()
     speeds = [speed_ref[i] for i in range(4)]
@@ -283,14 +314,15 @@
     tf0, tf1, ti0, ti1 = (rest[256 * i : 256 * i + 256, :] for i in range(4))
     ki, kf, kr = rest[1024:1280, :], rest[1280:1792, :], rest[1792:2048, 0:128]
     coltab, outtab = wide[0:256, :], wide[256:768, :]
-    pltpu.make_async_copy(r1, r1, recv_sem.at[0]).wait()
-    inverse = column_stage([r1[0], r1[1]], tf0, tf1, kr, ki, ti0, ti1, coltab, filters)
+    pltpu.make_async_copy(r1, r1, recv_sem.at[1]).wait()
+    groups = [jnp.concatenate([r1[2 * i + g] for i in range(8)], axis=0) for g in range(2)]
+    inverse = column_stage(groups, tf0, tf1, kr, ki, ti0, ti1, coltab, filters)
     e1[...] = half(inverse)
     swap = pltpu.make_async_remote_copy(
         src_ref=e1,
         dst_ref=e2,
-        send_sem=send_sem.at[2],
-        recv_sem=recv_sem.at[2],
+        send_sem=send_sem.at[3],
+        recv_sem=recv_sem.at[3],
         device_id=(1 - dist, me),
         device_id_type=MESH,
     )
@@ -299,9 +331,16 @@
     inverse = half(inverse + e2[...].astype(jnp.float32))
     m2[0] = inverse[0:128]
     m2[1] = inverse[128:256]
-    send_all(lambda t: m2.at[:, pl.ds(pl.multiple_of(2 * (t // 2), 2), 2), :], m2, r2, junk2, 1)
+    mine = r2.at[:, pl.ds(pl.multiple_of(32 * z + 8 * y + 2 * x, 2), 2), :]
+
+    def rows(t):
+        return m2.at[:, pl.ds(pl.multiple_of(2 * (t // 2), 2), 2), :]
+
+    far_first(me, lambda t: push(rows(t), mine, 1, 2, t))
+    pltpu.make_async_copy(rows(me), mine, recv_sem.at[2]).start()
+    pltpu.make_async_copy(rows(me), junk, send_sem.at[1]).start()
     big.wait()
-    pltpu.make_async_copy(r2, r2, recv_sem.at[1]).wait()
+    pltpu.make_async_copy(r2, r2, recv_sem.at[2]).wait()
     phase = last_stage([r2[0], r2[1]], tf0, tf1, kf, outtab)
     recon = half(recon_stage(phase, lambda a: weights[order_ref[0, a]]))
     parity = me % 2
@@ -312,7 +351,8 @@
     select = half(((source == offset + slot) & (slot < count)).astype(jnp.float32))
     out_ref[...] = half(dot(select, recon))
     swap.wait_send()
-    pltpu.make_async_copy(m1, m1, send_sem.at[0]).wait()
+    pltpu.make_async_copy(m1.at[pl.ds(0, 14)], b1.at[pl.ds(0, 14)], send_sem.at[0]).wait()
+    pltpu.make_async_copy(b1.at[pl.ds(0, 15)], r1.at[pl.ds(0, 15)], send_sem.at[2]).wait()
     pltpu.make_async_copy(r2, r2, send_sem.at[1]).wait()
 
 
@@ -334,21 +374,21 @@
             vmem(rowtab.shape, jnp.float32),
             vmem(rest.shape, lo),
             vmem(wide.shape, jnp.float32),
-            vmem((2, 256, 128), lo),
-            vmem((2, 256, 128), lo),
+            vmem((16, 32, 128), lo),
+            vmem((16, 32, 128), lo),
+            vmem((16, 32, 128), lo),
             vmem((2, 128, 128), lo),
             vmem((2, 256, 128), lo),
             vmem((256, 128), lo),
             vmem((256, 128), lo),
-            vmem((2, 2, 128), lo),
             vmem((2, 2, 128), lo),
             pltpu.SMEM(propagation.shape, jnp.float32),
             pltpu.SMEM(angle_order.shape, jnp.int32),
             pltpu.SMEM(slab_rows.shape, jnp.int32),
             pltpu.SemaphoreType.DMA((8,)),
             pltpu.SemaphoreType.DMA,
-            pltpu.SemaphoreType.DMA((3,)),
-            pltpu.SemaphoreType.DMA((3,)),
+            pltpu.SemaphoreType.DMA((4,)),
+            pltpu.SemaphoreType.DMA((4,)),
         ],
         compiler_params=pltpu.CompilerParams(collective_id=0, has_side_effects=True),
     )(holo, propagation, weights, angle_order, slab_rows, first, rowtab, rest, wide)

time: 31.7 us -> 31.1 us (0.981)
  Pallas kernels: 31 us -> 30.5 us
    pallas_call x1, Pallas kernels: 31 us -> 30.5 us  [on_device(): pl.pallas_call(kernel, out_shape=pltpu.VMEM((16, pixels), lo), in_specs=[...]
where the time goes in v4:
time: 31.1 us
  Pallas kernels  30.5 us (98%)
  local copies, waits for them, and re-layouts  0.61 us (2%)
    pallas_call x1, Pallas kernels, on_device(): pl.pallas_call(kernel, out_shape=pltpu.VMEM((16, pixels), lo), in_specs=[...  30.5 us

profile of v4, /device:TPU:1, one launch (start us, length us, event | category | flops | bytes accessed | tf_op | source)
XLA Modules:
  0.0 31.1 jit_solution(4056654676510140278)
XLA Ops:
  0.0 30.5 %shard_map.91 = bf16[16,512]{1,0:T(8,128)(2,1)S(1)} custom-call(bf16[64,1024]{1,0:T(8,128)(2,1)} %bitcast.1, f32[4]{0:T(128)} %speed_hbm.1, bf16[4,1024,512]{2,1,0:T(8,128)(2,1)} %weights_hbm.1, s32[1,4]{1,0:T(1,128)} %order_hbm.1, s32[128]{0:T(128)} %slab_hbm.1, bf16[256,512]{1,0:T(8,128)(2,1)} %constant.8.clone.first_hbm, ...), custom_call_target="tpu_custom_call" | custom-call | tf_op jit(solution)/shard_map/pallas_call | solution.py:365
  30.5 0.6 %copy.11 = bf16[16,512]{1,0:T(8,128)(2,1)} copy(bf16[16,512]{1,0:T(8,128)(2,1)S(1)} %shard_map.91) | data formatting | bytes 32768

commit v5 on v4

--- a/solution.py
+++ b/solution.py
@@ -211,27 +211,6 @@
     return me // 32, (me // 4) % 8, me % 4
 
 
-def far_first(me, act):
-    y, z, x = spot(me)
-    ys = [(y + i) % 4 * 32 for i in range(4)]
-    xs = [(x + i) % 4 for i in range(4)]
-    bases = {p: ys[p[0]] + xs[p[1]] for p in PLANE}
-
-    def layer(step, carry):
-        hop = (step + 1) // 2
-        at = (z + 4 + hop * (1 - 2 * (step % 2)) + 8) % 8 * 4
-        for p in PLANE:
-            act(bases[p] + at)
-
-        @pl.when(step < 7)
-        def _():
-            act(ys[0] + xs[0] + at)
-
-        return carry
-
-    lax.fori_loop(0, 8, layer, 0)
-
-
 def kernel(
     holo_hbm, speed_hbm, weights_hbm, order_hbm, slab_hbm, first_hbm, rowtab_hbm, rest_hbm, wide_hbm,
     out_ref,
@@ -274,13 +253,13 @@
             m1[2 * i + g] = spectrum[32 * i : 32 * i + 32, 128 * g : 128 * g + 128]
     pl.semaphore_wait(barrier, len(LINE) + len(PLANE) + 1)
 
-    def push(source, target, sent, landed, peer):
+    def push(source, target, sent, landed, peer, core=dist):
         pltpu.make_async_remote_copy(
             src_ref=source,
             dst_ref=target,
             send_sem=send_sem.at[sent],
             recv_sem=recv_sem.at[landed],
-            device_id=(dist, peer),
+            device_id=(core, peer),
             device_id_type=MESH,
         ).start()
 
@@ -336,9 +315,27 @@
     def rows(t):
         return m2.at[:, pl.ds(pl.multiple_of(2 * (t // 2), 2), 2), :]
 
-    far_first(me, lambda t: push(rows(t), mine, 1, 2, t))
-    pltpu.make_async_copy(rows(me), mine, recv_sem.at[2]).start()
-    pltpu.make_async_copy(rows(me), junk, send_sem.at[1]).start()
+    def layer(step, carry):
+        depth = 4 * dist + step
+        for core in (1, 0):
+            for at, to in plane:
+                t = at * 32 + depth * 4 + to
+                push(rows(t), mine, 1, 2, t, core)
+
+            @pl.when(jnp.logical_or(depth != z, dist != core))
+            def _():
+                t = y * 32 + depth * 4 + x
+                push(rows(t), mine, 1, 2, t, core)
+
+        return carry
+
+    lax.fori_loop(0, 4, layer, 0)
+
+    @pl.when(z // 4 == dist)
+    def _():
+        pltpu.make_async_copy(rows(me), mine, recv_sem.at[2]).start()
+        pltpu.make_async_copy(rows(me), junk, send_sem.at[1]).start()
+
     big.wait()
     pltpu.make_async_copy(r2, r2, recv_sem.at[2]).wait()
     phase = last_stage([r2[0], r2[1]], tf0, tf1, kf, outtab)

time: 31.1 us -> 29.6 us (0.952)
  Pallas kernels: 30.5 us -> 28.9 us
    pallas_call x1, Pallas kernels: 30.5 us -> 28.9 us  [on_device(): pl.pallas_call(kernel, out_shape=pltpu.VMEM((16, pixels), lo), in_specs=[...]
where the time goes in v5:
time: 29.6 us; the launch traced here: 29.5 us
  Pallas kernels  28.9 us (98%)
  local copies, waits for them, and re-layouts  0.61 us (2%)
    pallas_call x1, Pallas kernels, on_device(): pl.pallas_call(kernel, out_shape=pltpu.VMEM((16, pixels), lo), in_specs=[...  28.9 us
    unnamed x1, local copies, waits for them, and re-layouts  0.61 us

profile of v5, /device:TPU:1, one launch (start us, length us, event | category | flops | bytes accessed | tf_op | source)
XLA Modules:
  0.0 29.5 jit_solution(15158691881232079967)
XLA Ops:
  0.0 28.9 %shard_map.91 = bf16[16,512]{1,0:T(8,128)(2,1)S(1)} custom-call(bf16[64,1024]{1,0:T(8,128)(2,1)} %bitcast.1, f32[4]{0:T(128)} %speed_hbm.1, bf16[4,1024,512]{2,1,0:T(8,128)(2,1)} %weights_hbm.1, s32[1,4]{1,0:T(1,128)} %order_hbm.1, s32[128]{0:T(128)} %slab_hbm.1, bf16[256,512]{1,0:T(8,128)(2,1)} %constant.8.clone.first_hbm, ...), custom_call_target="tpu_custom_call" | custom-call | tf_op jit(solution)/shard_map/pallas_call | solution.py:362
  28.9 0.6 %copy.11 = bf16[16,512]{1,0:T(8,128)(2,1)} copy(bf16[16,512]{1,0:T(8,128)(2,1)S(1)} %shard_map.91) | data formatting | bytes 32768

commit v6 on v5

--- a/solution.py
+++ b/solution.py
@@ -35,23 +35,18 @@
     kr = np.concatenate([np.kron(np.eye(16), w) for w in wave], axis=0)
     ki = np.stack([np.einsum("ij,ab,d,my->iadmjby", np.eye(4), np.eye(4), np.ones(2), w) for w in wave])
     ki = np.moveaxis(ki, 0, 4).reshape(256, 256)
-    kf = [
-        np.einsum("ibx,ac,yz->biayxcz", w.reshape(4, 2, RADIX), np.eye(4), np.eye(8))
-        for w in wave
-    ]
-    kf = np.stack(kf).reshape(512, 256)
+    spectral = (8 * place[None, :] + short[:, None]).reshape(-1)
+    angle = turn * (np.outer(spectral, np.arange(N)) % N) / N
+    full = (np.cos(angle) + np.sin(angle)) * ROOT
+    perm = np.einsum("st,bc->sbct", np.eye(ROWS), eye2).reshape(256, 256)
     theta = turn * np.outer(short, long) / N
     rowtab = np.concatenate([np.cos(theta), np.sin(theta)], axis=0) * ROOT
-    lanes = np.arange(128)
-    tk = theta.T[:, lanes % RADIX]
+    tk = theta.T[:, np.arange(128) % RADIX]
     coltab = np.concatenate([np.cos(tk), np.sin(tk)], axis=0) * ROOT
-    tx = np.concatenate([theta.T[:, 2 * (lanes // 32) + b] for b in range(2)], axis=0)
-    outtab = np.concatenate([np.cos(tx), np.sin(tx)], axis=0) * ROOT
     first = np.concatenate(ts, axis=1)
-    rest = np.concatenate(tf + ti + [ki, kf, np.pad(kr, ((0, 0), (0, 128)))], axis=0)
+    rest = np.concatenate(tf + ti + [ki, perm, np.pad(kr, ((0, 0), (0, 128)))], axis=0)
     half = lambda v: np.asarray(v, np.float32).astype(jnp.bfloat16)
-    wide = np.concatenate([coltab, outtab], axis=0)
-    return half(first), rowtab.astype(np.float32), half(rest), wide.astype(np.float32)
+    return half(first), rowtab.astype(np.float32), half(full), half(rest), coltab.astype(np.float32)
 
 
 def dot(a, b):
@@ -173,37 +168,23 @@
     return dot(ti0, straight) + dot(ti1, turned)
 
 
-def last_stage(pair, tf0, tf1, kf, outtab):
-    cos, sin = outtab[0:256], outtab[256:512]
+def last_stage(pair, perm, weight_of):
     r = jnp.concatenate(pair, axis=1)
-    u, v = dot(tf0, r), dot(tf1, r)
-    rows = []
-    for p in range(2):
-        part = slice(128 * p, 128 * p + 128)
-        x, y = twist(cos, sin, u[:, part], v[:, part])
-        x, y = half(x), half(y)
-        rows.append(jnp.concatenate([x[0:128], x[128:256], y[0:128], y[128:256]], axis=1))
-    return dot(jnp.concatenate(rows, axis=0), kf)
-
-
-def recon_stage(phase, weight_of):
-    turned = [
-        [phase[128 * p : 128 * p + 128, 128 * g : 128 * g + 128].T for g in range(2)] for p in range(2)
-    ]
+    turned = lax.dot_general(r, perm, (((0,), (0,)), ((), ())), preferred_element_type=jnp.float32)
     total = None
     for a in range(4):
         tiles = []
-        for xm in range(RADIX):
-            g, at = xm // 4, ((xm % 4) * 4 + a) * 8
-            tiles.append(jnp.concatenate([turned[p][g][at : at + 8] for p in range(2)], axis=0))
-        lhs = half(jnp.concatenate(tiles, axis=1))
-        term = dot(lhs, weight_of(a))
+        for j in range(RADIX):
+            at, b = (j // 2 * 4 + a) * 8, j % 2 * 128
+            tiles.append(jnp.concatenate([turned[at + 128 * p : at + 128 * p + 8, b : b + 128] for p in range(2)], axis=0))
+        term = dot(half(jnp.concatenate(tiles, axis=1)), weight_of(a))
         total = term if total is None else total + term
     return total
 
 
 HOPS = [0, 1, 2, 1]
 PLANE = sorted(((i, j) for i in range(4) for j in range(4)), key=lambda p: -HOPS[p[0]] - HOPS[p[1]])[:-1]
+FIRST = 0
 LINE = [4, 3, 5, 2, 6, 1, 7]
 
 
@@ -212,10 +193,10 @@
 
 
 def kernel(
-    holo_hbm, speed_hbm, weights_hbm, order_hbm, slab_hbm, first_hbm, rowtab_hbm, rest_hbm, wide_hbm,
+    holo_hbm, speed_hbm, weights_hbm, order_hbm, slab_hbm, first_hbm, rowtab_hbm, full_hbm, rest_hbm, wide_hbm,
     out_ref,
-    holo, weights, first, rowtab, rest, wide, m1, b1, r1, m2, r2, e1, e2, junk, speed_ref, order_ref, slab_ref,
-    load_sem, weight_sem, send_sem, recv_sem,
+    holo, weights, spectral, first, rowtab, full, rest, wide, m1, b1, r1, m2, r2, e1, e2, junk, speed_ref, order_ref, slab_ref,
+    load_sem, weight_sem, send_sem, recv_sem, ready,
 ):
     dist = lax.axis_index("dist")
     me = lax.axis_index("rows")
@@ -227,7 +208,7 @@
     loads = [
         pltpu.make_async_copy(source, target, load_sem.at[i])
         for i, (source, target) in enumerate(
-            [(holo_hbm, holo), (first_hbm, first), (rowtab_hbm, rowtab), (rest_hbm, rest), (wide_hbm, wide),
+            [(holo_hbm, holo), (first_hbm, first), (rowtab_hbm, rowtab), (full_hbm, full), (rest_hbm, rest), (wide_hbm, wide),
              (speed_hbm, speed_ref), (order_hbm, order_ref), (slab_hbm, slab_ref)]
         )
     ]
@@ -236,10 +217,18 @@
     y, z, x = spot(me)
     line = [(z + i) % 8 for i in LINE]
     plane = [((y + i) % 4, (x + j) % 4) for i, j in PLANE]
-    for at in line:
-        greet(y * 32 + at * 4 + x)
+    late = z >= 4
+    first_plane = dist == FIRST
+    relaxed = jnp.logical_and(first_plane, z < 4)
+    telling = jnp.logical_and(first_plane, late)
     for at, to in plane:
         greet(at * 32 + z * 4 + to)
+    for at in line:
+
+        @pl.when(jnp.logical_or(jnp.logical_not(telling), at >= 4))
+        def _():
+            greet(y * 32 + at * 4 + x)
+
     pl.semaphore_signal(barrier, inc=1, device_id=(1 - dist, me), device_id_type=MESH)
     for load in loads[3:]:
         load.start()
@@ -251,7 +240,19 @@
     for i in range(8):
         for g in range(2):
             m1[2 * i + g] = spectrum[32 * i : 32 * i + 32, 128 * g : 128 * g + 128]
-    pl.semaphore_wait(barrier, len(LINE) + len(PLANE) + 1)
+
+    @pl.when(relaxed)
+    def _():
+        pl.semaphore_wait(barrier, len(PLANE) + 4)
+
+    @pl.when(jnp.logical_not(relaxed))
+    def _():
+        pl.semaphore_wait(barrier, len(PLANE) + 8)
+
+    @pl.when(telling)
+    def _():
+        for at in range(4):
+            pl.semaphore_signal(ready, inc=1, device_id=(dist, y * 32 + at * 4 + x), device_id_type=MESH)
 
     def push(source, target, sent, landed, peer, core=dist):
         pltpu.make_async_remote_copy(
@@ -278,21 +279,42 @@
             push(source.at[:, column(at, to), :], mine, 2, landed, at * 32 + z * 4 + to)
         pltpu.make_async_copy(source.at[:, column(y, x), :], mine, recv_sem.at[landed]).start()
 
-    for core, steps in enumerate([(along_line, in_plane), (in_plane, along_line)]):
-
-        @pl.when(dist == core)
-        def _():
-            steps[0](m1, b1, 0)
-            pltpu.make_async_copy(b1, b1, recv_sem.at[0]).wait()
-            steps[1](b1, r1, 1)
+    def transform(step, carry):
+        a, rows = step // 2, pl.ds(pl.multiple_of(step % 2 * 512, 512), 512)
+        spectral[a, rows, :] = half(dot(full[rows, :], weights[a]))
+        return carry
+
+    @pl.when(first_plane)
+    def _():
+        in_plane(m1, b1, 0)
+
+    @pl.when(jnp.logical_not(first_plane))
+    def _():
+        along_line(m1, b1, 0)
 
     for load in loads[3:]:
         load.wait()
+    big.wait()
+    lax.fori_loop(0, 4, transform, 0)
+    pltpu.make_async_copy(b1, b1, recv_sem.at[0]).wait()
+
+    @pl.when(relaxed)
+    def _():
+        pl.semaphore_wait(ready, 4)
+
+    @pl.when(first_plane)
+    def _():
+        along_line(b1, r1, 1)
+
+    @pl.when(jnp.logical_not(first_plane))
+    def _():
+        in_plane(b1, r1, 1)
+
     speeds = [speed_ref[i] for i in range(4)]
     filters = filter_stage(dist, me, speeds)
     tf0, tf1, ti0, ti1 = (rest[256 * i : 256 * i + 256, :] for i in range(4))
-    ki, kf, kr = rest[1024:1280, :], rest[1280:1792, :], rest[1792:2048, 0:128]
-    coltab, outtab = wide[0:256, :], wide[256:768, :]
+    ki, perm, kr = rest[1024:1280, :], rest[1280:1536, :], rest[1536:1792, 0:128]
+    coltab = wide[...]
     pltpu.make_async_copy(r1, r1, recv_sem.at[1]).wait()
     groups = [jnp.concatenate([r1[2 * i + g] for i in range(8)], axis=0) for g in range(2)]
     inverse = column_stage(groups, tf0, tf1, kr, ki, ti0, ti1, coltab, filters)
@@ -336,10 +358,9 @@
         pltpu.make_async_copy(rows(me), mine, recv_sem.at[2]).start()
         pltpu.make_async_copy(rows(me), junk, send_sem.at[1]).start()
 
-    big.wait()
+    lax.fori_loop(4, 8, transform, 0)
     pltpu.make_async_copy(r2, r2, recv_sem.at[2]).wait()
-    phase = last_stage([r2[0], r2[1]], tf0, tf1, kf, outtab)
-    recon = half(recon_stage(phase, lambda a: weights[order_ref[0, a]]))
+    recon = half(last_stage([r2[0], r2[1]], perm, lambda a: spectral[order_ref[0, a]]))
     parity = me % 2
     offset = parity * slab_ref[me - parity]
     count = slab_ref[me]
@@ -353,7 +374,7 @@
     pltpu.make_async_copy(r2, r2, send_sem.at[1]).wait()
 
 
-def on_device(first, rowtab, rest, wide, holograms, propagation, weights, angle_order, slab_rows):
+def on_device(first, rowtab, full, rest, wide, holograms, propagation, weights, angle_order, slab_rows):
     pixels = weights.shape[2]
     holo = holograms.reshape(64, N)
     anywhere = pl.BlockSpec(memory_space=pl.ANY)
@@ -362,13 +383,15 @@
     return pl.pallas_call(
         kernel,
         out_shape=pltpu.VMEM((16, pixels), lo),
-        in_specs=[anywhere] * 9,
+        in_specs=[anywhere] * 10,
         out_specs=pl.BlockSpec(memory_space=vmem),
         scratch_shapes=[
             vmem(holo.shape, lo),
             vmem(weights.shape, lo),
+            vmem(weights.shape, lo),
             vmem(first.shape, lo),
             vmem(rowtab.shape, jnp.float32),
+            vmem(full.shape, lo),
             vmem(rest.shape, lo),
             vmem(wide.shape, jnp.float32),
             vmem((16, 32, 128), lo),
@@ -382,13 +405,14 @@
             pltpu.SMEM(propagation.shape, jnp.float32),
             pltpu.SMEM(angle_order.shape, jnp.int32),
             pltpu.SMEM(slab_rows.shape, jnp.int32),
-            pltpu.SemaphoreType.DMA((8,)),
+            pltpu.SemaphoreType.DMA((9,)),
             pltpu.SemaphoreType.DMA,
             pltpu.SemaphoreType.DMA((4,)),
             pltpu.SemaphoreType.DMA((4,)),
+            pltpu.SemaphoreType.REGULAR,
         ],
         compiler_params=pltpu.CompilerParams(collective_id=0, has_side_effects=True),
-    )(holo, propagation, weights, angle_order, slab_rows, first, rowtab, rest, wide)
+    )(holo, propagation, weights, angle_order, slab_rows, first, rowtab, full, rest, wide)
 
 
 def solution(mesh):
@@ -398,7 +422,7 @@
         return jax.shard_map(
             on_device,
             mesh=mesh,
-            in_specs=(P(),) * 4
+            in_specs=(P(),) * 5
             + (P(None, None, "dist", "rows"), P(), P(None, None, "dist"), P(), P()),
             out_specs=P("rows", "dist"),
             check_vma=False,

time: 29.6 us -> 29 us (0.980)
  Pallas kernels: 28.9 us -> 28.3 us
    pallas_call x1, Pallas kernels: 28.9 us -> 28.3 us  [on_device(): pl.pallas_call(kernel, out_shape=pltpu.VMEM((16, pixels), lo), in_specs=[...]
where the time goes in v6:
time: 29 us
  Pallas kernels  28.3 us (98%)
  local copies, waits for them, and re-layouts  0.61 us (2%)
    pallas_call x1, Pallas kernels, on_device(): pl.pallas_call(kernel, out_shape=pltpu.VMEM((16, pixels), lo), in_specs=[...  28.3 us
    unnamed x1, local copies, waits for them, and re-layouts  0.61 us

profile of v6, /device:TPU:1, one launch (start us, length us, event | category | flops | bytes accessed | tf_op | source)
XLA Modules:
  0.0 29.0 jit_solution(4897768720374183003)
XLA Ops:
  0.0 28.3 %shard_map.100 = bf16[16,512]{1,0:T(8,128)(2,1)S(1)} custom-call(bf16[64,1024]{1,0:T(8,128)(2,1)} %bitcast.1, f32[4]{0:T(128)} %speed_hbm.1, bf16[4,1024,512]{2,1,0:T(8,128)(2,1)} %weights_hbm.1, s32[1,4]{1,0:T(1,128)} %order_hbm.1, s32[128]{0:T(128)} %slab_hbm.1, bf16[256,512]{1,0:T(8,128)(2,1)} %constant.10.clone.first_hbm, ...), custom_call_target="tpu_custom_call" | custom-call | tf_op jit(solution)/shard_map/pallas_call | solution.py:383
  28.4 0.6 %copy.12 = bf16[16,512]{1,0:T(8,128)(2,1)} copy(bf16[16,512]{1,0:T(8,128)(2,1)S(1)} %shard_map.100) | data formatting | bytes 32768

commit v7 on v6

--- a/solution.py
+++ b/solution.py
@@ -35,16 +35,15 @@
     kr = np.concatenate([np.kron(np.eye(16), w) for w in wave], axis=0)
     ki = np.stack([np.einsum("ij,ab,d,my->iadmjby", np.eye(4), np.eye(4), np.ones(2), w) for w in wave])
     ki = np.moveaxis(ki, 0, 4).reshape(256, 256)
-    spectral = (8 * place[None, :] + short[:, None]).reshape(-1)
+    spectral = (8 * place[None, :, None] + (2 * short[:4, None, None] + short[None, None, :2])).reshape(-1)
     angle = turn * (np.outer(spectral, np.arange(N)) % N) / N
     full = (np.cos(angle) + np.sin(angle)) * ROOT
-    perm = np.einsum("st,bc->sbct", np.eye(ROWS), eye2).reshape(256, 256)
     theta = turn * np.outer(short, long) / N
     rowtab = np.concatenate([np.cos(theta), np.sin(theta)], axis=0) * ROOT
     tk = theta.T[:, np.arange(128) % RADIX]
     coltab = np.concatenate([np.cos(tk), np.sin(tk)], axis=0) * ROOT
     first = np.concatenate(ts, axis=1)
-    rest = np.concatenate(tf + ti + [ki, perm, np.pad(kr, ((0, 0), (0, 128)))], axis=0)
+    rest = np.concatenate(tf + ti + [ki, np.pad(kr, ((0, 0), (0, 128)))], axis=0)
     half = lambda v: np.asarray(v, np.float32).astype(jnp.bfloat16)
     return half(first), rowtab.astype(np.float32), half(full), half(rest), coltab.astype(np.float32)
 
@@ -168,15 +167,14 @@
     return dot(ti0, straight) + dot(ti1, turned)
 
 
-def last_stage(pair, perm, weight_of):
-    r = jnp.concatenate(pair, axis=1)
-    turned = lax.dot_general(r, perm, (((0,), (0,)), ((), ())), preferred_element_type=jnp.float32)
+def last_stage(pair, weight_of):
+    turned = [r.astype(jnp.float32).T for r in pair]
     total = None
     for a in range(4):
         tiles = []
-        for j in range(RADIX):
-            at, b = (j // 2 * 4 + a) * 8, j % 2 * 128
-            tiles.append(jnp.concatenate([turned[at + 128 * p : at + 128 * p + 8, b : b + 128] for p in range(2)], axis=0))
+        for j in range(4):
+            at = (j * 4 + a) * 8
+            tiles.append(jnp.concatenate([half_turned[at : at + 8, :] for half_turned in turned], axis=0))
         term = dot(half(jnp.concatenate(tiles, axis=1)), weight_of(a))
         total = term if total is None else total + term
     return total
@@ -313,7 +311,7 @@
     speeds = [speed_ref[i] for i in range(4)]
     filters = filter_stage(dist, me, speeds)
     tf0, tf1, ti0, ti1 = (rest[256 * i : 256 * i + 256, :] for i in range(4))
-    ki, perm, kr = rest[1024:1280, :], rest[1280:1536, :], rest[1536:1792, 0:128]
+    ki, kr = rest[1024:1280, :], rest[1280:1536, 0:128]
     coltab = wide[...]
     pltpu.make_async_copy(r1, r1, recv_sem.at[1]).wait()
     groups = [jnp.concatenate([r1[2 * i + g] for i in range(8)], axis=0) for g in range(2)]
@@ -360,7 +358,7 @@
 
     lax.fori_loop(4, 8, transform, 0)
     pltpu.make_async_copy(r2, r2, recv_sem.at[2]).wait()
-    recon = half(last_stage([r2[0], r2[1]], perm, lambda a: spectral[order_ref[0, a]]))
+    recon = half(last_stage([r2[0], r2[1]], lambda a: spectral[order_ref[0, a]]))
     parity = me % 2
     offset = parity * slab_ref[me - parity]
     count = slab_ref[me]

time: 29 us -> 28.9 us (level)
  no operation moved by 1% of the time
where the time goes in v7:
time: 28.9 us; the launch traced here: 28.8 us
  Pallas kernels  28.2 us (98%)
  local copies, waits for them, and re-layouts  0.61 us (2%)
    pallas_call x1, Pallas kernels, on_device(): pl.pallas_call(kernel, out_shape=pltpu.VMEM((16, pixels), lo), in_specs=[...  28.2 us
    unnamed x1, local copies, waits for them, and re-layouts  0.61 us

profile of v7, /device:TPU:1, one launch (start us, length us, event | category | flops | bytes accessed | tf_op | source)
XLA Modules:
  0.0 28.8 jit_solution(14200149580941843236)
XLA Ops:
  0.0 28.2 %shard_map.100 = bf16[16,512]{1,0:T(8,128)(2,1)S(1)} custom-call(bf16[64,1024]{1,0:T(8,128)(2,1)} %bitcast.1, f32[4]{0:T(128)} %speed_hbm.1, bf16[4,1024,512]{2,1,0:T(8,128)(2,1)} %weights_hbm.1, s32[1,4]{1,0:T(1,128)} %order_hbm.1, s32[128]{0:T(128)} %slab_hbm.1, bf16[256,512]{1,0:T(8,128)(2,1)} %constant.10.clone.first_hbm, ...), custom_call_target="tpu_custom_call" | custom-call | tf_op jit(solution)/shard_map/pallas_call | solution.py:381
  28.2 0.6 %copy.12 = bf16[16,512]{1,0:T(8,128)(2,1)} copy(bf16[16,512]{1,0:T(8,128)(2,1)S(1)} %shard_map.100) | data formatting | bytes 32768

commit v8 on v7

--- a/solution.py
+++ b/solution.py
@@ -150,10 +150,11 @@
     return jnp.concatenate([table, table], axis=0)
 
 
-def column_stage(groups, tf0, tf1, kr, ki, ti0, ti1, coltab, filters):
+def column_stage(groups, tf, kr, ki, ti0, ti1, coltab, filters):
     cos, sin = twice(coltab[0:128]), twice(coltab[128:256])
     r = jnp.concatenate(groups, axis=1)
-    u, v = dot(tf0, r), dot(tf1, r)
+    both = dot(tf, r)
+    u, v = both[0:256], both[256:512]
     numer = []
     for g in range(2):
         part = slice(128 * g, 128 * g + 128)
@@ -310,12 +311,12 @@
 
     speeds = [speed_ref[i] for i in range(4)]
     filters = filter_stage(dist, me, speeds)
-    tf0, tf1, ti0, ti1 = (rest[256 * i : 256 * i + 256, :] for i in range(4))
+    tf, ti0, ti1 = rest[0:512, :], rest[512:768, :], rest[768:1024, :]
     ki, kr = rest[1024:1280, :], rest[1280:1536, 0:128]
     coltab = wide[...]
     pltpu.make_async_copy(r1, r1, recv_sem.at[1]).wait()
     groups = [jnp.concatenate([r1[2 * i + g] for i in range(8)], axis=0) for g in range(2)]
-    inverse = column_stage(groups, tf0, tf1, kr, ki, ti0, ti1, coltab, filters)
+    inverse = column_stage(groups, tf, kr, ki, ti0, ti1, coltab, filters)
     e1[...] = half(inverse)
     swap = pltpu.make_async_remote_copy(
         src_ref=e1,
@@ -357,14 +358,15 @@
         pltpu.make_async_copy(rows(me), junk, send_sem.at[1]).start()
 
     lax.fori_loop(4, 8, transform, 0)
-    pltpu.make_async_copy(r2, r2, recv_sem.at[2]).wait()
-    recon = half(last_stage([r2[0], r2[1]], lambda a: spectral[order_ref[0, a]]))
     parity = me % 2
     offset = parity * slab_ref[me - parity]
     count = slab_ref[me]
     slot = lax.broadcasted_iota(jnp.int32, (16, 16), 0)
     source = lax.broadcasted_iota(jnp.int32, (16, 16), 1)
     select = half(((source == offset + slot) & (slot < count)).astype(jnp.float32))
+    orders = [order_ref[0, a] for a in range(4)]
+    pltpu.make_async_copy(r2, r2, recv_sem.at[2]).wait()
+    recon = half(last_stage([r2[0], r2[1]], lambda a: spectral[orders[a]]))
     out_ref[...] = half(dot(select, recon))
     swap.wait_send()
     pltpu.make_async_copy(m1.at[pl.ds(0, 14)], b1.at[pl.ds(0, 14)], send_sem.at[0]).wait()

time: 28.9 us -> 29 us (level)
  no operation moved by 1% of the time
where the time goes in v8:
time: 29 us; the launch traced here: 28.9 us
  Pallas kernels  28.3 us (98%)
  local copies, waits for them, and re-layouts  0.61 us (2%)
    pallas_call x1, Pallas kernels, on_device(): pl.pallas_call(kernel, out_shape=pltpu.VMEM((16, pixels), lo), in_specs=[...  28.3 us
    unnamed x1, local copies, waits for them, and re-layouts  0.61 us

profile of v8, /device:TPU:1, one launch (start us, length us, event | category | flops | bytes accessed | tf_op | source)
XLA Modules:
  0.0 28.9 jit_solution(5972810280173070515)
XLA Ops:
  0.0 28.3 %shard_map.100 = bf16[16,512]{1,0:T(8,128)(2,1)S(1)} custom-call(bf16[64,1024]{1,0:T(8,128)(2,1)} %bitcast.1, f32[4]{0:T(128)} %speed_hbm.1, bf16[4,1024,512]{2,1,0:T(8,128)(2,1)} %weights_hbm.1, s32[1,4]{1,0:T(1,128)} %order_hbm.1, s32[128]{0:T(128)} %slab_hbm.1, bf16[256,512]{1,0:T(8,128)(2,1)} %constant.10.clone.first_hbm, ...), custom_call_target="tpu_custom_call" | custom-call | tf_op jit(solution)/shard_map/pallas_call | solution.py:383
  28.3 0.6 %copy.12 = bf16[16,512]{1,0:T(8,128)(2,1)} copy(bf16[16,512]{1,0:T(8,128)(2,1)S(1)} %shard_map.100) | data formatting | bytes 32768
